TPU v7x, 32 devices: a whole 2x2x4 slice. The times are simulated.
32 devices in a mesh: dp: 4 (over z), ctx: 8 (over y, x, core).
Axes of the slice: x: 2, y: 2, z: 4, core: 2. Of those that a mesh axis runs over, the one named last changes fastest.
Arguments:
- inputs: bfloat16 [4, 2048, 4096], P('dp', 'ctx'), may hold values from -6 to 6
- value_weight: bfloat16 [4096, 512], P('ctx'), may hold values from -0.09375 to 0.09375
- query_states: bfloat16 [4, 2048, 2048], P('dp', 'ctx'), may hold values from -40 to 40
- key_states: bfloat16 [4, 2048, 512], P('dp', 'ctx'), may hold values from -6 to 6
- value_states: bfloat16 [4, 2048, 512], P('dp', 'ctx'), may hold values from -6 to 6
- attention_out: bfloat16 [4, 2048, 2048], P('dp', 'ctx'), may hold values from -4 to 4
- out_grad: bfloat16 [4, 2048, 2048], P('dp', 'ctx'), may hold values from -6 to 6
- segment_ids: int32 [4, 2048], P('dp', 'ctx'), may hold values from 0 to 3, never falling along the last dimension, each value on 1 to 1024 neighbouring positions
Outputs:
- query_grad: bfloat16 [4, 2048, 2048], P('dp', 'ctx')
- key_grad: bfloat16 [4, 2048, 512], P('dp', 'ctx')
- input_grad: bfloat16 [4, 2048, 4096], P('dp', 'ctx')
- weight_grad: float32 [4096, 512], P('ctx')
Inputs may be any that keep to these rules, and one draw needn't show every extreme that they name: `segment_ids`: along each sequence the ids never fall; each record holds 1 to 1024 tokens and one holds exactly 1024.
All inputs are finite; a program needn't handle non-finite values.
Results may differ from a plain program's by a relative error of at most 0.0057.
Values may be sent and summed in bfloat16 or wider, within the bound.
No kernel may reach another device: no remote copies, remote signals or barrier semaphores. Data moves between devices by JAX's collectives and lax.ppermute only.
A program may use at most 128 MiB of HBM per device.

v0:
```python
import math

import jax
import jax.numpy as jnp
from jax import lax
from jax.sharding import PartitionSpec as P

HQ = 16
KVH = 4
DH = 128
W = 2048


def carried_in(value, axis, combine, identity):
    peers, here = (lax.axis_size(axis), lax.axis_index(axis))
    everything = jax.tree.map(lambda part: lax.all_gather(part, axis), value)
    start = jax.tree.map(
        lambda part, zero: jnp.broadcast_to(jnp.asarray(zero, part.dtype), part.shape),
        value,
        identity,
    )

    def turn(k, before):
        reached = k < here
        new = combine(before, jax.tree.map(lambda part: part[k], everything))
        return jax.tree.map(lambda a, b: jnp.where(reached, a, b), new, before)

    return lax.fori_loop(0, peers, turn, start)


def passed_along(block, axis, distance):
    devices = range(lax.axis_size(axis))
    route = [(i - distance, i) for i in devices if i - distance in devices]
    return lax.ppermute(block, axis, route)


def link_records(earlier, later):
    first_early, last_early, start_early, whole_early, empty_early = earlier
    first_late, last_late, start_late, whole_late, empty_late = later
    joined = last_early == first_late
    start_merged = jnp.where((whole_late == 1) & joined, start_early, start_late)
    whole_merged = jnp.where((whole_early == 1) & (whole_late == 1) & joined, 1, 0).astype(
        jnp.int32
    )
    merged = (first_early, last_late, start_merged, whole_merged, jnp.zeros_like(empty_early))
    return tuple(
        (
            jnp.where(
                empty_early == 1, late_item, jnp.where(empty_late == 1, early_item, merged_item)
            )
            for early_item, late_item, merged_item in zip(earlier, later, merged)
        )
    )


def attend_group(operands, live_mask, factor):
    query_group, key_group, value_group, grad_group, output_group = operands
    scores = (
        jnp.einsum("gqd,kd->gqk", query_group, key_group, preferred_element_type=jnp.float32)
        * factor
    )
    scores = jnp.where(live_mask[None], scores, -1e30)
    row_max = jnp.max(scores, axis=-1, keepdims=True)
    exp_score = jnp.exp(scores - row_max)
    prob_full = exp_score / jnp.sum(exp_score, axis=-1, keepdims=True)
    prob_low = prob_full.astype(jnp.bfloat16)
    row_delta = jnp.sum(
        grad_group.astype(jnp.float32) * output_group.astype(jnp.float32), axis=-1, keepdims=True
    )
    prob_grad = jnp.einsum(
        "gqd,kd->gqk", grad_group, value_group, preferred_element_type=jnp.float32
    )
    score_grad = (prob_full * (prob_grad - row_delta)).astype(jnp.bfloat16)
    query_part = (
        jnp.einsum("gqk,kd->gqd", score_grad, key_group, preferred_element_type=jnp.float32)
        * factor
    )
    key_part = (
        jnp.einsum("gqk,gqd->kd", score_grad, query_group, preferred_element_type=jnp.float32)
        * factor
    )
    value_part = jnp.einsum("gqk,gqd->kd", prob_low, grad_group, preferred_element_type=jnp.float32)
    return (query_part, key_part, value_part)


def attend_tail(factor, operands):
    query_heads, key_heads, value_heads, grad_heads, output_heads, live_mask = operands
    query_part, key_part, value_part = lax.map(
        lambda head_parts: attend_group(head_parts, live_mask, factor),
        (query_heads, key_heads, value_heads, grad_heads, output_heads),
    )
    return (query_part, key_part, value_part)


def on_device(
    inputs,
    value_weight,
    query_states,
    key_states,
    value_states,
    attention_out,
    out_grad,
    segment_ids,
):
    tok_rows = query_states.shape[1]
    span_blocks = W // tok_rows
    group_size = HQ // KVH
    width_kv = KVH * DH
    factor = 1.0 / math.sqrt(DH)
    window_rows = (span_blocks + 1) * tok_rows
    input_rows = inputs[0]
    values = value_states[0]
    seg_local = segment_ids[0]
    device_index = lax.axis_index("ctx")
    offset = device_index * tok_rows
    before = jnp.sum((seg_local[None, :] < seg_local[:, None]).astype(jnp.int32), axis=1)
    first_id = seg_local[0]
    last_id = seg_local[-1]
    summary = (
        first_id,
        last_id,
        offset + before[-1],
        (first_id == last_id).astype(jnp.int32),
        jnp.zeros((), jnp.int32),
    )
    identity = tuple((jnp.full((), filler, jnp.int32) for filler in (0, 0, 0, 1, 1)))
    prior = carried_in(summary, "ctx", link_records, identity)
    carried = (before == 0) & (prior[4] == 0) & (prior[1] == first_id)
    starts = jnp.where(carried, prior[2], offset + before)
    kv_block = jnp.stack([key_states[0], values])
    doubling_plan = []
    window = kv_block
    blocks_held = 1
    while blocks_held < span_blocks + 1:
        needed = min(blocks_held, span_blocks + 1 - blocks_held)
        received = passed_along(window[:, (blocks_held - needed) * tok_rows :], "ctx", blocks_held)
        window = jnp.concatenate([received, window], axis=1)
        doubling_plan.append((blocks_held, needed))
        blocks_held = blocks_held + needed
    key_base = offset - span_blocks * tok_rows
    key_pos = key_base + jnp.arange(window_rows, dtype=jnp.int32)
    query_pos = offset + jnp.arange(tok_rows, dtype=jnp.int32)
    live_mask = (
        (key_pos[None, :] >= starts[:, None])
        & (key_pos[None, :] <= query_pos[:, None])
        & (key_pos[None, :] > query_pos[:, None] - W)
    )
    query_heads = query_states[0].reshape(tok_rows, KVH, group_size, DH).transpose(1, 2, 0, 3)
    grad_heads = out_grad[0].reshape(tok_rows, KVH, group_size, DH).transpose(1, 2, 0, 3)
    output_heads = attention_out[0].reshape(tok_rows, KVH, group_size, DH).transpose(1, 2, 0, 3)
    key_heads = window[0].reshape(window_rows, KVH, DH).transpose(1, 0, 2)
    value_heads = window[1].reshape(window_rows, KVH, DH).transpose(1, 0, 2)
    operands = (query_heads, key_heads, value_heads, grad_heads, output_heads, live_mask)
    query_part, key_part, value_part = attend_tail(factor, operands)
    query_grad = query_part.transpose(2, 0, 1, 3).reshape(1, tok_rows, HQ * DH).astype(jnp.bfloat16)
    grads = jnp.stack(
        [
            key_part.transpose(1, 0, 2).reshape(window_rows, width_kv),
            value_part.transpose(1, 0, 2).reshape(window_rows, width_kv),
        ]
    )
    for blocks_held, needed in reversed(doubling_plan):
        sent = grads[:, : needed * tok_rows]
        kept_rows = grads[:, needed * tok_rows :]
        returned = passed_along(sent, "ctx", -blocks_held)
        split_at = (blocks_held - needed) * tok_rows
        grads = jnp.concatenate(
            [kept_rows[:, :split_at], kept_rows[:, split_at:] + returned], axis=1
        )
    key_grad = grads[0].astype(jnp.bfloat16)[None]
    value_delta = grads[1].astype(jnp.bfloat16)
    input_grad = jnp.einsum(
        "tk,rk->tr",
        value_delta,
        lax.all_gather(value_weight, "ctx", axis=0, tiled=True),
        preferred_element_type=jnp.float32,
    )
    input_grad = input_grad.astype(jnp.bfloat16)[None]
    weight_share = lax.psum_scatter(
        jnp.einsum("tr,tk->rk", input_rows, value_delta, preferred_element_type=jnp.float32),
        "ctx",
        scatter_dimension=0,
        tiled=True,
    )
    weight_grad = lax.psum(weight_share, "dp")
    return (query_grad, key_grad, input_grad, weight_grad)


def solution(mesh):
    placed = (
        P("dp", "ctx", None),
        P("ctx", None),
        P("dp", "ctx", None),
        P("dp", "ctx", None),
        P("dp", "ctx", None),
        P("dp", "ctx", None),
        P("dp", "ctx", None),
        P("dp", "ctx"),
    )
    return jax.shard_map(
        on_device,
        mesh=mesh,
        in_specs=placed,
        out_specs=(
            P("dp", "ctx", None),
            P("dp", "ctx", None),
            P("dp", "ctx", None),
            P("ctx", None),
        ),
        check_vma=False,
    )
```

profile of v0, /device:TPU:0, one launch (start us, length us, event | category | flops | bytes accessed | tf_op | source)
XLA Modules:
  0.0 681.1 jit_solution(11382272146703181672)
XLA Ops:
  14.6 11.5 %collective-permute-start.2 = (bf16[2,512,512]{1,2,0:T(8,128)(2,1)S(1)}, bf16[2,512,512]{1,2,0:T(8,128)(2,1)S(1)}, u32[]{:S(2)}, u32[]{:S(2)}) collective-permute-start(bf16[2,512,512]{1,2,0:T(8,128)(2,1)S(1)} %maximum_maximum_fusion.1), channel_id=1, source_target_pairs={{0,2},{1,3},{2,4},{3,5},{4,6},{5,7},{8,10},{9,11},{10,12},{11,13},... | collective-permute-start | bytes 3145736 | tf_op jit(solution)/shard_map/ppermute | solution.py:34
  26.1 21.7 %collective-permute-done.2 = bf16[2,512,512]{1,2,0:T(8,128)(2,1)S(1)} collective-permute-done((bf16[2,512,512]{1,2,0:T(8,128)(2,1)S(1)}, bf16[2,512,512]{1,2,0:T(8,128)(2,1)S(1)}, u32[]{:S(2)}, u32[]{:S(2)}) %collective-permute-start.2) | collective-permute-done | bytes 1048608 | tf_op jit(solution)/shard_map/ppermute | solution.py:34
  50.5 6.7 collective-permute-start.3
  67.4 31.2 %all-reduce.5 = (s32[8]{0:T(128)S(1)}, s32[8]{0:T(128)S(1)}, s32[8]{0:T(128)S(1)}, s32[8]{0:T(128)S(1)}, s32[8]{0:T(128)S(1)}) all-reduce(s32[8]{0:T(128)S(1)} %bitcast_dynamic-update-slice_fusion.1, s32[8]{0:T(128)S(1)} %dynamic-update-slice.1, s32[8]{0:T(128)S(1)} %dynamic-update-slice.2, ...), channel_id=2, replica_groups=mesh['dp'=4,'ctx'=8] {'ctx'}, use_global_device_ids=true, to_apply=%add | all-reduce | flops 40 | bytes 320 | tf_op jit(solution)/shard_map/all_gather | solution.py:16
  98.6 66.3 %while.32 = (s32[]{:T(128)}, s32[]{:T(128)}, s32[]{:T(128)}, s32[]{:T(128)}, s32[]{:T(128)}, /*index=5*/s32[8]{0:T(128)S(1)}, s32[8]{0:T(128)S(1)}, s32[8]{0:T(1...) while((s32[]{:T(128)}, s32[]{:T(128)}, s32[]{:T(128)}, s32[]{:T(128)}, ...), condition=%wide.region_2.3_spmd, body=%wide.region_1.2_spmd.sunk | while | flops 18 | bytes 363 | solution.py:28
  178.1 120.7 %while.33 = (s32[]{:T(128)}, bf16[4,4,256,128]{3,2,1,0:T(8,128)(2,1)}, f32[4,2304,128]{2,1,0:T(8,128)}, f32[4,2304,128]{2,1,0:T(8,128)}, bf16[4,4,256,128]{2,3,1...) while((s32[]{:T(128)}, ...), condition=%wide.region_7.8_spmd.clone, body=%wide.region_3.7_spmd.clone.sunk | while | flops 3658453504 | bytes 52402368 | solution.py:88
  180.5 8.4 %fusion.118 = (f32[4,256]{1,0:T(4,128)S(1)}, f32[4,256,2304]{2,1,0:T(8,128)}) fusion(pred[256,2304]{1,0:T(8,128)(4,1)S(1)} %compare_and_fusion.2, bf16[4,2304,128]{1,2,0:T(8,128)(2,1)} %get-tuple-element.586, s32[]{:T(128)} %get-tuple-element.567, bf16[4,4,256,128]{2,3,1,0:T(8,128)(2,1)} %get-tuple-element.585), kind=kOutput, calls=%fused_computation.87.clone.1 | convolution fusion | flops 613419264 | bytes 10884096 | tf_op jit(solution)/shard_map/while/body/eval_jaxpr/sub | solution.py:64
  201.4 6.8 fusion.121
  210.7 8.4 %fusion.118 = (f32[4,256]{1,0:T(4,128)S(1)}, f32[4,256,2304]{2,1,0:T(8,128)}) fusion(pred[256,2304]{1,0:T(8,128)(4,1)S(1)} %compare_and_fusion.2, bf16[4,2304,128]{1,2,0:T(8,128)(2,1)} %get-tuple-element.586, s32[]{:T(128)} %get-tuple-element.567, bf16[4,4,256,128]{2,3,1,0:T(8,128)(2,1)} %get-tuple-element.585), kind=kOutput, calls=%fused_computation.87.clone.1 | convolution fusion | flops 613419264 | bytes 10884096 | tf_op jit(solution)/shard_map/while/body/eval_jaxpr/sub | solution.py:64
  231.5 6.8 %fusion.121 = f32[4,2304,128]{2,1,0:T(8,128)} fusion(f32[4,2304,128]{2,1,0:T(8,128)} %get-tuple-element.570, s32[]{:T(128)} %get-tuple-element.567, f32[4,256]{1,0:T(4,128)S(1)} %get-tuple-element.513, pred[256,2304]{1,0:T(8,128)(4,1)S(1)} %compare_and_fusion.2, bf16[4,2304,128]{1,2,0:T(8,128)(2,1)} %get-tuple-element.586, ...), kind=kOutput, calls=%fused_computation.17.clone.1 | convolution fusion | flops 1219759360 | bytes 2889728 | tf_op jit(solution)/shard_map/while/body/eval_jaxpr/gqk,gqd->kd/dot_general | solution.py:82
  240.8 8.4 %fusion.118 = (f32[4,256]{1,0:T(4,128)S(1)}, f32[4,256,2304]{2,1,0:T(8,128)}) fusion(pred[256,2304]{1,0:T(8,128)(4,1)S(1)} %compare_and_fusion.2, bf16[4,2304,128]{1,2,0:T(8,128)(2,1)} %get-tuple-element.586, s32[]{:T(128)} %get-tuple-element.567, bf16[4,4,256,128]{2,3,1,0:T(8,128)(2,1)} %get-tuple-element.585), kind=kOutput, calls=%fused_computation.87.clone.1 | convolution fusion | flops 613419264 | bytes 10884096 | tf_op jit(solution)/shard_map/while/body/eval_jaxpr/sub | solution.py:64
  261.8 6.8 fusion.121
  271.0 8.4 %fusion.118 = (f32[4,256]{1,0:T(4,128)S(1)}, f32[4,256,2304]{2,1,0:T(8,128)}) fusion(pred[256,2304]{1,0:T(8,128)(4,1)S(1)} %compare_and_fusion.2, bf16[4,2304,128]{1,2,0:T(8,128)(2,1)} %get-tuple-element.586, s32[]{:T(128)} %get-tuple-element.567, bf16[4,4,256,128]{2,3,1,0:T(8,128)(2,1)} %get-tuple-element.585), kind=kOutput, calls=%fused_computation.87.clone.1 | convolution fusion | flops 613419264 | bytes 10884096 | tf_op jit(solution)/shard_map/while/body/eval_jaxpr/sub | solution.py:64
  279.4 5.4 multiply_convert_fusion.2
  291.9 6.8 %fusion.121 = f32[4,2304,128]{2,1,0:T(8,128)} fusion(f32[4,2304,128]{2,1,0:T(8,128)} %get-tuple-element.570, s32[]{:T(128)} %get-tuple-element.567, f32[4,256]{1,0:T(4,128)S(1)} %get-tuple-element.513, pred[256,2304]{1,0:T(8,128)(4,1)S(1)} %compare_and_fusion.2, bf16[4,2304,128]{1,2,0:T(8,128)(2,1)} %get-tuple-element.586, ...), kind=kOutput, calls=%fused_computation.17.clone.1 | convolution fusion | flops 1219759360 | bytes 2889728 | tf_op jit(solution)/shard_map/while/body/eval_jaxpr/gqk,gqd->kd/dot_general | solution.py:82
  298.7 11.1 %copy.47 = f32[2304,4,128]{2,1,0:T(4,128)} copy(f32[2304,4,128]{2,0,1:T(8,128)} %bitcast.169) | data formatting | bytes 9437184 | tf_op jit(solution)/shard_map/transpose | solution.py:158
  309.8 6.6 stack_reshape.6
  321.6 10.9 %copy.48 = f32[2304,4,128]{2,1,0:T(4,128)} copy(f32[2304,4,128]{2,0,1:T(8,128)S(1)} %bitcast.172) | data formatting | bytes 9437184 | tf_op jit(solution)/shard_map/transpose | solution.py:159
  332.5 6.5 stack_reshape.7
  351.8 86.6 %collective-permute-done.5 = f32[2,1024,512]{2,1,0:T(8,128)} collective-permute-done((f32[2,1024,512]{2,1,0:T(8,128)S(1)}, f32[2,1024,512]{2,1,0:T(8,128)}, u32[]{:S(2)}, u32[]{:S(2)}) %collective-permute-start.5) | collective-permute-done | bytes 4194336 | tf_op jit(solution)/shard_map/ppermute | solution.py:34
  443.1 43.9 %collective-permute-done.6 = f32[2,512,512]{2,1,0:T(8,128)S(1)} collective-permute-done((f32[2,512,512]{2,1,0:T(8,128)S(1)}, f32[2,512,512]{2,1,0:T(8,128)S(1)}, u32[]{:S(2)}, u32[]{:S(2)}) %collective-permute-start.6) | collective-permute-done | bytes 2097184 | tf_op jit(solution)/shard_map/ppermute | solution.py:34
  498.6 80.7 %reduce-scatter.2.cloned.1.call-done = f32[512,512]{0,1:T(8,128)} async-done(((f32[4096,512]{0,1:T(8,128)}), f32[512,512]{0,1:T(8,128)}) %reduce-scatter.2.cloned.1.call-update) | async-done | bytes 1048592 | tf_op jit(solution)/shard_map/reduce_scatter | solution.py:179
  584.6 33.2 %all-gather.4.cloned.1.call-done = bf16[4096,512]{1,0:T(8,128)(2,1)} async-done(((bf16[512,512]{1,0:T(8,128)(2,1)}), bf16[4096,512]{1,0:T(8,128)(2,1)}) %all-gather.4.cloned.1.call-update) | async-done | bytes 4194320 | tf_op jit(solution)/shard_map/all_gather | solution.py:175
  622.7 49.4 %all-reduce.8.cloned.1.call-done = f32[512,512]{0,1:T(8,128)} async-done(((f32[512,512]{0,1:T(8,128)}), f32[512,512]{0,1:T(8,128)}) %all-reduce.8.cloned.1.call-update) | async-done | bytes 1048592 | tf_op jit(solution)/shard_map/psum | solution.py:185
  (174 shorter events, 157.3 us)
Async XLA Ops:
  7.2 486.1 %copy-start = (bf16[1,256,4096]{2,1,0:T(8,128)(2,1)S(1)}, bf16[1,256,4096]{2,1,0:T(8,128)(2,1)}, u32[]{:S(2)}) copy-start(bf16[1,256,4096]{2,1,0:T(8,128)(2,1)} %param.12) | copy-start | bytes 6291460
  7.2 54.1 %copy-start.8 = (u32[32]{0:T(128)S(1)}, u32[32]{0:T(128)}, u32[]{:S(2)}) copy-start(u32[32]{0:T(128)} %constant.81) | copy-start | bytes 388
  7.2 51.4 %copy-start.7 = (s32[1,256]{1,0:T(1,128)S(1)}, s32[1,256]{1,0:T(1,128)}, u32[]{:S(2)}) copy-start(s32[1,256]{1,0:T(1,128)} %param.19) | copy-start | bytes 3076
  7.2 572.1 %reduce-scatter.2.cloned.1.call-start = ((), (), s32[]{:S(2)}) async-start(), calls=%async_computation.2 | async-start | bytes 9437184 | tf_op jit(solution)/shard_map/reduce_scatter | solution.py:179
  10.4 4.1 collective-permute-start.1
  14.6 33.3 %collective-permute-start.2 = (bf16[2,512,512]{1,2,0:T(8,128)(2,1)S(1)}, bf16[2,512,512]{1,2,0:T(8,128)(2,1)S(1)}, u32[]{:S(2)}, u32[]{:S(2)}) collective-permute-start(bf16[2,512,512]{1,2,0:T(8,128)(2,1)S(1)} %maximum_maximum_fusion.1), channel_id=1, source_target_pairs={{0,2},{1,3},{2,4},{3,5},{4,6},{5,7},{8,10},{9,11},{10,12},{11,13},... | collective-permute-start | bytes 3145736 | tf_op jit(solution)/shard_map/ppermute | solution.py:34
  50.5 123.1 %collective-permute-start.3 = (bf16[2,1024,512]{1,2,0:T(8,128)(2,1)}, bf16[2,1024,512]{1,2,0:T(8,128)(2,1)}, u32[]{:S(2)}, u32[]{:S(2)}) collective-permute-start(bf16[2,1024,512]{1,2,0:T(8,128)(2,1)} %maximum_maximum_fusion), channel_id=1, source_target_pairs={{0,4},{1,5},{2,6},{3,7},{8,12},{9,13},{10,14},{11,15},{16,20},{17,... | collective-permute-start | bytes 6291464 | tf_op jit(solution)/shard_map/ppermute | solution.py:34
  57.1 115.3 %collective-permute-start = (bf16[2,256,512]{1,2,0:T(8,128)(2,1)}, bf16[2,256,512]{1,2,0:T(8,128)(2,1)}, u32[]{:S(2)}, u32[]{:S(2)}) collective-permute-start(bf16[2,256,512]{1,2,0:T(8,128)(2,1)} %pad_maximum_fusion.1), channel_id=1, source_target_pairs={} | collective-permute-start | bytes 1572872 | tf_op jit(solution)/shard_map/ppermute | solution.py:34
  172.4 3.0 copy-start.3
  194.4 3.5 copy-start.5
  200.4 1.0 copy-start.6
  224.5 3.5 copy-start.5
  230.6 1.0 copy-start.6
  254.7 3.6 copy-start.5
  284.8 3.5 copy-start.5
  309.8 11.8 %slice-start = ((s8[4718592]{0:T(1024)(128)(4,1)}), s8[524288]{0:T(1024)(128)(4,1)S(1)}, s32[]{:S(2)}) async-start(s8[4718592]{0:T(1024)(128)(4,1)} %bitcast.170), calls=%async_computation.4 | async-start | bytes 1048576
  316.4 5.2 slice-start.1
  344.1 6.7 copy-start.1
  346.9 91.5 %collective-permute-start.5 = (f32[2,1024,512]{2,1,0:T(8,128)S(1)}, f32[2,1024,512]{2,1,0:T(8,128)}, u32[]{:S(2)}, u32[]{:S(2)}) collective-permute-start(f32[2,1024,512]{2,1,0:T(8,128)S(1)} %slice.82), channel_id=1, source_target_pairs={{4,0},{5,1},{6,2},{7,3},{12,8},{13,9},{14,10},{15,11},{20,16},{21,... | collective-permute-start | bytes 12582920 | tf_op jit(solution)/shard_map/ppermute | solution.py:34
  349.8 1.9 collective-permute-start.4
  441.8 45.2 %collective-permute-start.6 = (f32[2,512,512]{2,1,0:T(8,128)S(1)}, f32[2,512,512]{2,1,0:T(8,128)S(1)}, u32[]{:S(2)}, u32[]{:S(2)}) collective-permute-start(f32[2,512,512]{2,1,0:T(8,128)S(1)} %slice.84), channel_id=1, source_target_pairs={{2,0},{3,1},{4,2},{5,3},{6,4},{7,5},{10,8},{11,9},{12,10},{13,11},... | collective-permute-start | bytes 6291464 | tf_op jit(solution)/shard_map/ppermute | solution.py:34
  487.6 4.6 collective-permute-start.7
  497.8 120.0 %all-gather.4.cloned.1.call-start = ((), (), s32[]{:S(2)}) async-start(), calls=%async_computation.1 | async-start | bytes 4718592 | tf_op jit(solution)/shard_map/all_gather | solution.py:175
  498.5 173.5 %all-reduce.8.cloned.1.call-start = ((), (), s32[]{:S(2)}) async-start(), calls=%async_computation.3 | async-start | bytes 2097152 | tf_op jit(solution)/shard_map/psum | solution.py:185
  (4 other events, 3.7 us)
Sparse Core Ops, SparseCore 0:
  497.9 81.3 reduce-scatter.1
  581.1 36.5 all-gather.3
  620.1 51.8 all-reduce.7
where the time goes:
time: 683 us; the launch traced here: 681 us
  waiting for transfers between devices  321 us (47%)
  local copies, waits for them, and re-layouts  117 us (17%)
  matrix products  116 us (17%)
  loops' own time  40.9 us (6%)
  blocking collectives  31.2 us (5%)
  starting transfers between devices  27.3 us (4%)
  between operations  16.6 us (2%)
  other arithmetic  11.1 us (2%)
    ppermute x8, waiting for transfers between devices, passed_along(): return lax.ppermute(block, axis, route)  157 us
    reduce_scatter x1, waiting for transfers between devices, on_device(): lax.psum_scatter(jnp.einsum('tr,tk->rk', input_rows, value_delta, preferr...  80.7 us
    psum x1, waiting for transfers between devices, on_device(): weight_grad = lax.psum(weight_share, 'dp')  49.4 us
    another operation x1, loops' own time, carried_in(): return lax.fori_loop(0, peers, turn, start)  40.7 us
    sub x4, matrix products, attend_group(): exp_score = jnp.exp(scores - row_max)  33.5 us
    all_gather x1, waiting for transfers between devices, on_device(): lax.all_gather(value_weight, 'ctx', axis=0, tiled=True)  33.2 us
    all_gather x1, blocking collectives, carried_in(): everything = jax.tree.map(lambda part: lax.all_gather(part, axis), value)  31.2 us
    dot_general x4, matrix products, attend_group(): jnp.einsum('gqk,gqd->kd', prob_low, grad_group, preferred_element_type=jn...  27.2 us
  transfers between devices with their start and end apart: 11, of which 8 were waited for; matrix products, arithmetic and copies ran while one was open for 8% of the time, Pallas kernels for 0%

commit v1 on v0

v1 whole, which is shorter than its diff:
```python
import functools
import math

import jax
import jax.numpy as jnp
from jax import lax
from jax.experimental import pallas as pl
from jax.experimental.pallas import tpu as pltpu
from jax.sharding import PartitionSpec as P

HQ = 16
KVH = 4
DH = 128
W = 2048
GROUP = HQ // KVH
NEG = -1e30
SEG_ROWS = 16
BF16 = jnp.bfloat16
F32 = jnp.float32


def nt_dot(a, b):
    return lax.dot_general(a, b, (((1,), (1,)), ((), ())), preferred_element_type=F32)


def nn_dot(a, b):
    return lax.dot_general(a, b, (((1,), (0,)), ((), ())), preferred_element_type=F32)


def tn_dot(a, b):
    return lax.dot_general(a, b, (((0,), (0,)), ((), ())), preferred_element_type=F32)


def attend_kernel(chips_back, tok, idx_ref, *refs):
    blocks = chips_back + 1
    slots = 2 * blocks
    q_ref, grad_ref, out_ref = refs[:3]
    same_refs = refs[3 : 3 + blocks]
    sib_refs = refs[3 + blocks : 3 + 2 * blocks]
    same_seg = refs[3 + 2 * blocks : 3 + 3 * blocks]
    sib_seg = refs[3 + 3 * blocks : 3 + 4 * blocks]
    dq_ref, same_out, sib_out = refs[3 + 4 * blocks : 6 + 4 * blocks]
    (win, key_t, q4, g4, exp_s, max_s, acc, dq_t, prob_s, ds_s, low_s, lo_s) = refs[
        6 + 4 * blocks :
    ]
    head = pl.program_id(0)
    here = idx_ref[0]
    core = lax.rem(here, 2)
    chip = lax.div(here, 2)
    base0 = 2 * (chip - chips_back) * tok
    own_slot = 2 * chips_back + core
    factor = 1.0 / math.sqrt(DH)
    scale = factor * math.log2(math.e)
    iota_k = lax.broadcasted_iota(jnp.int32, (tok, tok), 0)
    iota_q = lax.broadcasted_iota(jnp.int32, (tok, tok), 1)

    def slot_of(d, which):
        return 2 * (chips_back - d) + which

    @pl.when(head == 0)
    def _():
        mine = same_seg[0][0:1, 0:tok].astype(F32)
        count = jnp.zeros((1, tok), F32)
        for d in range(blocks):
            for which, seg in ((core, same_seg[d]), (1 - core, sib_seg[d])):
                row = seg[0:1, 0:tok].astype(F32)
                column = jnp.broadcast_to(row, (tok, tok)).T
                below = jnp.sum(jnp.where(column < mine, 1.0, 0.0), axis=0, keepdims=True)
                valid = (chip >= d).astype(F32)
                count = count + below * valid
        start = count.astype(jnp.int32) + jnp.maximum(base0, 0)
        query_pos = here * tok + lax.broadcasted_iota(jnp.int32, (1, tok), 1)
        low = jnp.maximum(start, query_pos - (W - 1))
        low_s[...] = jnp.broadcast_to(low, low_s.shape)
        lo_s[0] = lax.div(jnp.min(low.astype(F32)).astype(jnp.int32) - base0, tok)

    for d in range(blocks):
        for which, ref in ((core, same_refs[d]), (1 - core, sib_refs[d])):
            slot = slot_of(d, which)
            win[slot] = ref[...]
            key_t[slot] = ref[0:tok, :].T
    acc[...] = jnp.zeros_like(acc)
    dq_t[...] = jnp.zeros_like(dq_t)
    deltas = []
    for h in range(GROUP):
        cols = slice(h * DH, (h + 1) * DH)
        rows = slice(h * tok, (h + 1) * tok)
        q4[rows] = q_ref[:, cols]
        g4[rows] = grad_ref[:, cols]
        prod = grad_ref[:, cols].astype(F32) * out_ref[:, cols].astype(F32)
        deltas.append(jnp.sum(prod.T, axis=0, keepdims=True))
    low = low_s[0:1]

    def first(t, carry, diagonal):
        keys = win[t, 0:tok]
        bound = low - (base0 + t * tok)
        keep = iota_k >= bound
        if diagonal:
            keep = keep & (iota_k <= iota_q)
        maxes, sums = carry
        new_maxes, new_sums = [], []
        for h in range(GROUP):
            rows = slice(h * tok, (h + 1) * tok)
            s = jnp.where(keep, nt_dot(keys, q4[rows]), NEG)
            m = jnp.maximum(maxes[h], jnp.max(s, axis=0, keepdims=True))
            e = jnp.exp2((s - m) * scale)
            exp_s[t, :, rows] = e
            max_s[t, h : h + 1] = m
            new_maxes.append(m)
            new_sums.append(
                sums[h] * jnp.exp2((maxes[h] - m) * scale) + jnp.sum(e, axis=0, keepdims=True)
            )
        return tuple(new_maxes), tuple(new_sums)

    lo = lo_s[0]
    empty = (
        tuple(jnp.full((1, tok), NEG, F32) for _ in range(GROUP)),
        tuple(jnp.zeros((1, tok), F32) for _ in range(GROUP)),
    )
    stats = lax.fori_loop(lo, own_slot, lambda t, c: first(t, c, False), empty)
    maxes, sums = first(own_slot, stats, True)
    inverse = [1.0 / total for total in sums]

    def second(t, carry):
        values = win[t, tok : 2 * tok]
        for h in range(GROUP):
            rows = slice(h * tok, (h + 1) * tok)
            weight = jnp.exp2((max_s[t, h : h + 1] - maxes[h]) * scale) * inverse[h]
            prob = exp_s[t, :, rows] * weight
            prob_grad = nt_dot(values, g4[rows])
            ds_s[:, rows] = (prob * (prob_grad - deltas[h])).astype(BF16)
            prob_s[:, rows] = prob.astype(BF16)
        acc[t, tok : 2 * tok] = nn_dot(prob_s[...], g4[...])
        acc[t, 0:tok] = nn_dot(ds_s[...], q4[...]) * factor
        dq_t[...] += nn_dot(key_t[t], ds_s[...])
        return carry

    lax.fori_loop(lo, own_slot + 1, second, 0)
    for h in range(GROUP):
        rows = slice(h * tok, (h + 1) * tok)
        dq_ref[:, h * DH : (h + 1) * DH] = (dq_t[:, rows].T * factor).astype(BF16)
    for d in range(blocks):
        same_out[d] = acc[slot_of(d, core)]
        sib_out[d] = acc[slot_of(d, 1 - core)].astype(BF16)


def attend(index, query, grad, output, same, sibling):
    tok = query.shape[0]
    blocks = len(same)
    slots = 2 * blocks
    width = KVH * DH
    wide = GROUP * DH
    rows = GROUP * tok
    head_spec = pl.BlockSpec((tok, wide), lambda g, s: (0, g))
    kv_spec = pl.BlockSpec((2 * tok, DH), lambda g, s: (0, g))
    seg_spec = pl.BlockSpec((SEG_ROWS, width), lambda g, s: (2 * tok // SEG_ROWS, 0))
    part_spec = pl.BlockSpec((blocks, 2 * tok, DH), lambda g, s: (0, 0, g))
    pairs = tok * (blocks * 2 - 1) * tok * HQ
    return pl.pallas_call(
        functools.partial(attend_kernel, blocks - 1, tok),
        grid_spec=pltpu.PrefetchScalarGridSpec(
            num_scalar_prefetch=1,
            grid=(KVH,),
            in_specs=[head_spec] * 3 + [kv_spec] * slots + [seg_spec] * slots,
            out_specs=[head_spec, part_spec, part_spec],
            scratch_shapes=[
                pltpu.VMEM((slots, 2 * tok, DH), BF16),
                pltpu.VMEM((slots, DH, tok), BF16),
                pltpu.VMEM((rows, DH), BF16),
                pltpu.VMEM((rows, DH), BF16),
                pltpu.VMEM((slots, tok, rows), F32),
                pltpu.VMEM((slots, 8, tok), F32),
                pltpu.VMEM((slots, 2 * tok, DH), F32),
                pltpu.VMEM((DH, rows), F32),
                pltpu.VMEM((tok, rows), BF16),
                pltpu.VMEM((tok, rows), BF16),
                pltpu.VMEM((8, tok), jnp.int32),
                pltpu.SMEM((1,), jnp.int32),
            ],
        ),
        out_shape=[
            jax.ShapeDtypeStruct((tok, HQ * DH), BF16),
            jax.ShapeDtypeStruct((blocks, 2 * tok, width), F32),
            jax.ShapeDtypeStruct((blocks, 2 * tok, width), BF16),
        ],
        cost_estimate=pl.CostEstimate(
            flops=20 * pairs * DH, bytes_accessed=12 << 20, transcendentals=pairs
        ),
        name="attend",
    )(index, query, grad, output, *same, *sibling, *same, *sibling)


def weight_kernel(count, *refs):
    out_ref = refs[2 * count]
    for s in range(count):
        part = tn_dot(refs[s][...], refs[count + s][...])
        if s == 0:
            out_ref[...] = part
        else:
            out_ref[...] += part


def weight_product(rows, deltas):
    count = len(rows)
    tok, depth = rows[0].shape
    width = deltas[0].shape[1]
    return pl.pallas_call(
        functools.partial(weight_kernel, count),
        out_shape=jax.ShapeDtypeStruct((depth, width), F32),
        cost_estimate=pl.CostEstimate(
            flops=2 * count * tok * depth * width,
            bytes_accessed=count * tok * (depth + width) * 2 + depth * width * 4,
            transcendentals=0,
        ),
        name="weight_product",
    )(*rows, *deltas)


def shifted(block, axis, distance):
    devices = range(lax.axis_size(axis))
    route = [(i, i + distance) for i in devices if i + distance in devices]
    return lax.ppermute(block, axis, route)


def swapped(block, axis, mask):
    return lax.ppermute(block, axis, [(i, i ^ mask) for i in range(lax.axis_size(axis))])


def gathered(block, axis):
    size = lax.axis_size(axis)
    even = [block if m == 0 else swapped(block, axis, m) for m in range(0, size, 2)]
    odd = swapped(jnp.stack(even), axis, 1)
    return [(even[m // 2] if m % 2 == 0 else odd[m // 2]) for m in range(size)]


def summed(part, axis):
    size = lax.axis_size(axis)
    here = lax.axis_index(axis)
    masks = []
    mask = 1
    while mask < size:
        masks.append(mask)
        mask *= 2
    for mask in masks[:-1]:
        half = part.shape[0] // 2
        bit = (here // mask) % 2
        keep = lax.dynamic_slice_in_dim(part, bit * half, half, 0)
        send = lax.dynamic_slice_in_dim(part, (1 - bit) * half, half, 0)
        part = keep + swapped(send.astype(BF16), axis, mask).astype(F32)
    if masks:
        low = part.astype(BF16)
        part = low.astype(F32) + swapped(low, axis, masks[-1]).astype(F32)
    for mask in reversed(masks[:-1]):
        low = part.astype(BF16)
        other = swapped(low, axis, mask)
        bit = (here // mask) % 2
        part = jnp.concatenate(
            [jnp.where(bit == 0, low, other), jnp.where(bit == 0, other, low)]
        ).astype(F32)
    return part


def input_kernel(count, idx_ref, delta_ref, *refs):
    out_ref = refs[count]
    delta = delta_ref[...]
    depth = refs[0].shape[0]
    for s in range(count):
        column = pl.multiple_of((idx_ref[0] ^ s) * depth, depth)
        out_ref[:, pl.ds(column, depth)] = nt_dot(delta, refs[s][...]).astype(BF16)


def input_product(index, delta, weights):
    count = len(weights)
    tok, width = delta.shape
    depth = weights[0].shape[0]
    if depth % 128:
        full = jnp.stack(weights)
        order = jnp.arange(count) ^ index[0]
        full = jnp.take(full, order, axis=0).reshape(count * depth, width)
        product = jnp.einsum("tk,rk->tr", delta, full, preferred_element_type=F32)
        return product.astype(BF16)
    vmem = pl.BlockSpec(memory_space=pltpu.VMEM)
    return pl.pallas_call(
        functools.partial(input_kernel, count),
        in_specs=[pl.BlockSpec(memory_space=pltpu.SMEM)] + [vmem] * (1 + count),
        out_specs=vmem,
        out_shape=jax.ShapeDtypeStruct((tok, count * depth), BF16),
        cost_estimate=pl.CostEstimate(
            flops=2 * count * tok * depth * width,
            bytes_accessed=count * depth * (width + tok) * 2,
            transcendentals=0,
        ),
        name="input_product",
    )(index, delta, *weights)


def on_device(
    inputs,
    value_weight,
    query_states,
    key_states,
    value_states,
    attention_out,
    out_grad,
    segment_ids,
):
    size = lax.axis_size("ctx")
    here = lax.axis_index("ctx")
    tok = query_states.shape[1]
    depth = value_weight.shape[0]
    width = KVH * DH
    index = here.astype(jnp.int32).reshape(1)
    reach = min(W, size * tok // 2)
    chips_back = -(-(-(-(reach - 1) // tok)) // 2)
    seg = jnp.pad(segment_ids.astype(BF16), ((0, SEG_ROWS - 1), (0, width - tok)))
    own = jnp.concatenate([key_states[0], value_states[0], seg], axis=0)
    same = [own] + [shifted(own, "ctx", 2 * d) for d in range(1, chips_back + 1)]
    sibling = [swapped(block, "ctx", 1) for block in same]
    query_grad, same_part, sib_part = attend(
        index, query_states[0], out_grad[0], attention_out[0], same, sibling
    )
    rows = [
        lax.dynamic_slice_in_dim(inputs[0], (here ^ m) * depth, depth, 1) for m in range(size)
    ]
    rows = [rows[0]] + [swapped(rows[m], "ctx", m) for m in range(1, size)]
    weights = gathered(value_weight, "ctx")

    part = swapped(sib_part, "ctx", 1)
    total = same_part[0] + part[0].astype(F32)
    for d in range(1, chips_back + 1):
        chip_sum = (same_part[d] + part[d].astype(F32)).astype(BF16)
        total = total + shifted(chip_sum, "ctx", -2 * d).astype(F32)
    low = total.astype(BF16)
    key_grad = low[:tok]
    value_delta = low[tok:]
    deltas = gathered(value_delta, "ctx")
    weight_grad = summed(weight_product(rows, deltas), "dp")
    input_grad = input_product(index, value_delta, weights)
    return (query_grad[None], key_grad[None], input_grad[None], weight_grad)


def solution(mesh):
    placed = (
        P("dp", "ctx", None),
        P("ctx", None),
        P("dp", "ctx", None),
        P("dp", "ctx", None),
        P("dp", "ctx", None),
        P("dp", "ctx", None),
        P("dp", "ctx", None),
        P("dp", "ctx"),
    )
    return jax.shard_map(
        on_device,
        mesh=mesh,
        in_specs=placed,
        out_specs=(
            P("dp", "ctx", None),
            P("dp", "ctx", None),
            P("dp", "ctx", None),
            P("ctx", None),
        ),
        check_vma=False,
    )
```

time: 683 us -> 210 us (0.31)
  waiting for transfers between devices: 321 us -> 118 us
  matrix products: 116 us -> 0 us
  local copies, waits for them, and re-layouts: 117 us -> 10.5 us
  loops' own time: 40.9 us -> 0 us
  blocking collectives: 31.2 us -> 0 us
  starting transfers between devices: 27.3 us -> 49.2 us
  Pallas kernels: 0 us -> 20 us
  between operations: 16.6 us -> 0.93 us
    dot_general x18 -> x0, matrix products: 82.6 us -> none  [the longest x4 27.2 us: attend_group(): jnp.einsum('gqk,gqd->kd', prob_low, grad_group, preferred_element_type=jn...]
    reduce_scatter x1 -> x0, waiting for transfers between devices: 80.7 us -> none  [on_device(): lax.psum_scatter(jnp.einsum('tr,tk->rk', input_rows, value_delta, preferr...]
    psum x1 -> x0, waiting for transfers between devices: 49.4 us -> none  [on_device(): weight_grad = lax.psum(weight_share, 'dp')]
    another operation x2 -> x0, loops' own time: 40.9 us -> none  [the longest x1 40.7 us: carried_in(): return lax.fori_loop(0, peers, turn, start)]
    ppermute x8 -> x26, waiting for transfers between devices: 157 us -> 118 us  [the longest x22 77.4 us: swapped(): lax.ppermute(block, axis, [(i, i ^ mask) for i in range(lax.axis_size(axi...]
    sub x4 -> x0, matrix products: 33.5 us -> none  [attend_group(): exp_score = jnp.exp(scores - row_max)]
    all_gather x1 -> x0, waiting for transfers between devices: 33.2 us -> none  [on_device(): lax.all_gather(value_weight, 'ctx', axis=0, tiled=True)]
    all_gather x1 -> x0, blocking collectives: 31.2 us -> none  [carried_in(): everything = jax.tree.map(lambda part: lax.all_gather(part, axis), value)]
  transfers between devices with their start and end apart: 11 -> 26, of which waited for: 8 -> 18; matrix products, arithmetic and copies ran while one was open for 8% -> 5% of each run, Pallas kernels for 0% -> 4%
where the time goes in v1:
time: 210 us; the launch traced here: 209 us
  waiting for transfers between devices  118 us (56%)
  starting transfers between devices  49.2 us (23%)
  Pallas kernels  20 us (10%)
  local copies, waits for them, and re-layouts  10.5 us (5%)
  other arithmetic  10.3 us (5%)
    ppermute x22, waiting for transfers between devices, swapped(): lax.ppermute(block, axis, [(i, i ^ mask) for i in range(lax.axis_size(axi...  77.4 us
    ppermute x4, waiting for transfers between devices, shifted(): return lax.ppermute(block, axis, route)  40.8 us
    ppermute x22, starting transfers between devices, swapped(): lax.ppermute(block, axis, [(i, i ^ mask) for i in range(lax.axis_size(axi...  38.1 us
    ppermute x4, starting transfers between devices, shifted(): return lax.ppermute(block, axis, route)  11 us
    pallas_call x1, Pallas kernels, attend(): pl.pallas_call(functools.partial(attend_kernel, blocks - 1, tok), grid_sp...  10.7 us
    squeeze x2, local copies, waits for them, and re-layouts, gathered(): return [even[m // 2] if m % 2 == 0 else odd[m // 2] for m in range(size)]  5.14 us
    pallas_call x1, Pallas kernels, input_product(): pl.pallas_call(functools.partial(input_kernel, count), in_specs=[pl.Block...  4.83 us
    pallas_call x1, Pallas kernels, weight_product(): pl.pallas_call(functools.partial(weight_kernel, count), out_shape=jax.Sha...  4.38 us
  transfers between devices with their start and end apart: 26, of which 18 were waited for; matrix products, arithmetic and copies ran while one was open for 5% of the time, Pallas kernels for 4%

profile of v1, /device:TPU:0, one launch (start us, length us, event | category | flops | bytes accessed | tf_op | source)
XLA Modules:
  0.0 209.0 jit_solution(2118557703651635404)
XLA Ops:
  2.4 4.9 %collective-permute-start = (bf16[528,512]{1,0:T(8,128)(2,1)S(1)}, bf16[528,512]{1,0:T(8,128)(2,1)S(1)}, u32[]{:S(2)}, u32[]{:S(2)}) collective-permute-start(bf16[528,512]{1,0:T(8,128)(2,1)S(1)} %fusion.3.refs_3_.refs_9_), channel_id=1, source_target_pairs={{0,2},{1,3},{2,4},{3,5},{4,6},{5,7},{8,10},{9,11},{10,12},{11,13},... | collective-permute-start | bytes 1622024 | tf_op jit(solution)/shard_map/ppermute | solution.py:222
  7.3 3.4 %collective-permute-start.1 = (bf16[528,512]{1,0:T(8,128)(2,1)S(1)}, bf16[528,512]{1,0:T(8,128)(2,1)S(1)}, u32[]{:S(2)}, u32[]{:S(2)}) collective-permute-start(bf16[528,512]{1,0:T(8,128)(2,1)S(1)} %fusion.3.refs_3_.refs_9_), channel_id=1, source_target_pairs={{0,4},{1,5},{2,6},{3,7},{8,12},{9,13},{10,14},{11,15},{16,20},{17,... | collective-permute-start | bytes 1622024 | tf_op jit(solution)/shard_map/ppermute | solution.py:222
  10.8 8.0 %collective-permute-done.refs_4_.refs_10_ = bf16[528,512]{1,0:T(8,128)(2,1)S(1)} collective-permute-done((bf16[528,512]{1,0:T(8,128)(2,1)S(1)}, bf16[528,512]{1,0:T(8,128)(2,1)S(1)}, u32[]{:S(2)}, u32[]{:S(2)}) %collective-permute-start) | collective-permute-done | bytes 540704 | tf_op jit(solution)/shard_map/ppermute | solution.py:222
  18.8 12.5 %collective-permute-done.1.refs_5_.refs_11_ = bf16[528,512]{1,0:T(8,128)(2,1)S(1)} collective-permute-done((bf16[528,512]{1,0:T(8,128)(2,1)S(1)}, bf16[528,512]{1,0:T(8,128)(2,1)S(1)}, u32[]{:S(2)}, u32[]{:S(2)}) %collective-permute-start.1) | collective-permute-done | bytes 540704 | tf_op jit(solution)/shard_map/ppermute | solution.py:222
  34.0 10.7 %attend.1 = (bf16[256,2048]{1,0:T(8,128)(2,1)}, f32[3,512,512]{2,1,0:T(8,128)}, bf16[3,512,512]{2,1,0:T(8,128)(2,1)}) custom-call(s32[1]{0:T(128)} %bitcast.idx_ref, bf16[256,2048]{1,0:T(8,128)(2,1)} %bitcast.71, bf16[256,2048]{1,0:T(8,128)(2,1)} %bitcast.72, bf16[256,2048]{1,0:T(8,128)(2,1)} %bitcast.73, bf16[528,512]{1,0:T(8,128)(2,1)} %copy-done.9, ...), custom_call_target="tpu_custom_call" | custom-call | flops 13421772800 | bytes 12582912 | tf_op jit(solution)/shard_map/attend/pallas_call | solution.py:159
  44.8 4.9 %collective-permute-start.5 = (bf16[3,512,512]{2,1,0:T(8,128)(2,1)}, bf16[3,512,512]{2,1,0:T(8,128)(2,1)S(1)}, u32[]{:S(2)}, u32[]{:S(2)}) collective-permute-start(bf16[3,512,512]{2,1,0:T(8,128)(2,1)} %get-tuple-element.9), channel_id=1, source_target_pairs={{0,1},{1,0},{2,3},{3,2},{4,5},{5,4},{6,7},{7,6},{8,9},{9,8},{10,11... | collective-permute-start | bytes 4718600 | tf_op jit(solution)/shard_map/ppermute | solution.py:226
  49.7 3.2 %collective-permute-done.5 = bf16[3,512,512]{2,1,0:T(8,128)(2,1)S(1)} collective-permute-done((bf16[3,512,512]{2,1,0:T(8,128)(2,1)}, bf16[3,512,512]{2,1,0:T(8,128)(2,1)S(1)}, u32[]{:S(2)}, u32[]{:S(2)}) %collective-permute-start.5) | collective-permute-done | bytes 1572896 | tf_op jit(solution)/shard_map/ppermute | solution.py:226
  57.7 13.4 %collective-permute-done.6 = bf16[512,512]{1,0:T(8,128)(2,1)S(1)} collective-permute-done((bf16[512,512]{1,0:T(8,128)(2,1)S(1)}, bf16[512,512]{1,0:T(8,128)(2,1)S(1)}, u32[]{:S(2)}, u32[]{:S(2)}) %collective-permute-start.6) | collective-permute-done | bytes 524320 | tf_op jit(solution)/shard_map/ppermute | solution.py:222
  71.0 6.9 %collective-permute-done.7 = bf16[512,512]{1,0:T(8,128)(2,1)S(1)} collective-permute-done((bf16[512,512]{1,0:T(8,128)(2,1)S(1)}, bf16[512,512]{1,0:T(8,128)(2,1)S(1)}, u32[]{:S(2)}, u32[]{:S(2)}) %collective-permute-start.7) | collective-permute-done | bytes 524320 | tf_op jit(solution)/shard_map/ppermute | solution.py:222
  80.3 11.3 %collective-permute-start.19 = (bf16[256,512]{1,0:T(8,128)(2,1)S(1)}, bf16[256,512]{1,0:T(8,128)(2,1)S(1)}, u32[]{:S(2)}, u32[]{:S(2)}) collective-permute-start(bf16[256,512]{1,0:T(8,128)(2,1)S(1)} %get-tuple-element.31.delta_ref.refs_8_), channel_id=1, source_target_pairs={{0,2},{1,3},{2,0},{3,1},{4,6},{5,7},{6,4},{7,5},{8,10},{9,11},{10,... | collective-permute-start | bytes 786440 | tf_op jit(solution)/shard_map/ppermute | solution.py:226
  95.1 3.7 %collective-permute-done.19.refs_10_ = bf16[256,512]{1,0:T(8,128)(2,1)S(1)} collective-permute-done((bf16[256,512]{1,0:T(8,128)(2,1)S(1)}, bf16[256,512]{1,0:T(8,128)(2,1)S(1)}, u32[]{:S(2)}, u32[]{:S(2)}) %collective-permute-start.19) | collective-permute-done | bytes 262176 | tf_op jit(solution)/shard_map/ppermute | solution.py:226
  99.8 6.6 %collective-permute-done.20.refs_12_ = bf16[256,512]{1,0:T(8,128)(2,1)S(1)} collective-permute-done((bf16[256,512]{1,0:T(8,128)(2,1)S(1)}, bf16[256,512]{1,0:T(8,128)(2,1)S(1)}, u32[]{:S(2)}, u32[]{:S(2)}) %collective-permute-start.20) | collective-permute-done | bytes 262176 | tf_op jit(solution)/shard_map/ppermute | solution.py:226
  107.5 8.1 %collective-permute-done.8.refs_2_ = bf16[512,512]{1,0:T(8,128)(2,1)S(1)} collective-permute-done((bf16[512,512]{1,0:T(8,128)(2,1)S(1)}, bf16[512,512]{1,0:T(8,128)(2,1)S(1)}, u32[]{:S(2)}, u32[]{:S(2)}) %collective-permute-start.8) | collective-permute-done | bytes 524320 | tf_op jit(solution)/shard_map/ppermute | solution.py:226
  115.6 12.0 %collective-permute-done.9.refs_4_ = bf16[512,512]{1,0:T(8,128)(2,1)S(1)} collective-permute-done((bf16[512,512]{1,0:T(8,128)(2,1)S(1)}, bf16[512,512]{1,0:T(8,128)(2,1)S(1)}, u32[]{:S(2)}, u32[]{:S(2)}) %collective-permute-start.9) | collective-permute-done | bytes 524320 | tf_op jit(solution)/shard_map/ppermute | solution.py:226
  134.4 6.2 %collective-permute-done.13.refs_2_ = bf16[256,512]{1,0:T(8,128)(2,1)S(1)} collective-permute-done((bf16[256,512]{1,0:T(8,128)(2,1)S(1)}, bf16[256,512]{1,0:T(8,128)(2,1)S(1)}, u32[]{:S(2)}, u32[]{:S(2)}) %collective-permute-start.13) | collective-permute-done | bytes 262176 | tf_op jit(solution)/shard_map/ppermute | solution.py:226
  140.6 4.7 %collective-permute-done.14.refs_3_ = bf16[256,512]{1,0:T(8,128)(2,1)S(1)} collective-permute-done((bf16[256,512]{1,0:T(8,128)(2,1)S(1)}, bf16[256,512]{1,0:T(8,128)(2,1)S(1)}, u32[]{:S(2)}, u32[]{:S(2)}) %collective-permute-start.14) | collective-permute-done | bytes 262176 | tf_op jit(solution)/shard_map/ppermute | solution.py:226
  150.4 4.9 %collective-permute-done.17.refs_6_ = bf16[256,512]{1,0:T(8,128)(2,1)S(1)} collective-permute-done((bf16[256,512]{1,0:T(8,128)(2,1)S(1)}, bf16[256,512]{1,0:T(8,128)(2,1)S(1)}, u32[]{:S(2)}, u32[]{:S(2)}) %collective-permute-start.17) | collective-permute-done | bytes 262176 | tf_op jit(solution)/shard_map/ppermute | solution.py:226
  155.3 4.8 %collective-permute-done.18.refs_7_ = bf16[256,512]{1,0:T(8,128)(2,1)S(1)} collective-permute-done((bf16[256,512]{1,0:T(8,128)(2,1)S(1)}, bf16[256,512]{1,0:T(8,128)(2,1)S(1)}, u32[]{:S(2)}, u32[]{:S(2)}) %collective-permute-start.18) | collective-permute-done | bytes 262176 | tf_op jit(solution)/shard_map/ppermute | solution.py:226
  160.9 4.4 %weight_product.1 = f32[512,512]{1,0:T(8,128)} custom-call(bf16[256,512]{1,0:T(8,128)(2,1)} %get-tuple-element.18.refs_0_, bf16[256,512]{1,0:T(8,128)(2,1)} %copy-done.10, bf16[256,512]{1,0:T(8,128)(2,1)} %copy-done.11, bf16[256,512]{1,0:T(8,128)(2,1)} %copy-done.12, bf16[256,512]{1,0:T(8,128)(2,1)} %copy-done.13, bf16[256,512]{1,0:T(8,128)(2,1)} %copy-done.14, ...), custom_call_target="tpu_custom_call" | custom-call | flops 1073741824 | bytes 5242880 | tf_op jit(solution)/shard_map/weight_product/pallas_call | solution.py:207
  166.4 8.4 %collective-permute-done.23 = bf16[256,512]{1,0:T(8,128)(2,1)S(1)} collective-permute-done((bf16[256,512]{1,0:T(8,128)(2,1)S(1)}, bf16[256,512]{1,0:T(8,128)(2,1)S(1)}, u32[]{:S(2)}, u32[]{:S(2)}) %collective-permute-start.23) | collective-permute-done | bytes 262176 | tf_op jit(solution)/shard_map/ppermute | solution.py:226
  175.9 12.1 %collective-permute-start.24 = (bf16[256,512]{1,0:T(8,128)(2,1)S(1)}, bf16[256,512]{1,0:T(8,128)(2,1)S(1)}, u32[]{:S(2)}, u32[]{:S(2)}) collective-permute-start(bf16[256,512]{1,0:T(8,128)(2,1)S(1)} %add_convert_fusion.3), channel_id=1, source_target_pairs={{0,16},{8,24},{16,0},{24,8},{1,17},{9,25},{17,1},{25,9},{2,18},{10... | collective-permute-start | bytes 786440 | tf_op jit(solution)/shard_map/ppermute | solution.py:226
  188.0 11.4 %collective-permute-done.24 = bf16[256,512]{1,0:T(8,128)(2,1)S(1)} collective-permute-done((bf16[256,512]{1,0:T(8,128)(2,1)S(1)}, bf16[256,512]{1,0:T(8,128)(2,1)S(1)}, u32[]{:S(2)}, u32[]{:S(2)}) %collective-permute-start.24) | collective-permute-done | bytes 262176 | tf_op jit(solution)/shard_map/ppermute | solution.py:226
  199.6 2.9 %slice_bitcast_fusion = (bf16[512,512]{1,0:T(8,128)(2,1)}, bf16[512,512]{1,0:T(8,128)(2,1)}, bf16[512,512]{1,0:T(8,128)(2,1)}, bf16[512,512]{1,0:T(8,128)(2,1)}) fusion(bf16[4,512,512]{2,1,0:T(8,128)(2,1)} %collective-permute-done.11), kind=kLoop, calls=%fused_computation.12 | loop fusion | bytes 4194304 | tf_op jit(solution)/shard_map/squeeze | solution.py:233
  202.5 4.8 %input_product.1 = bf16[256,4096]{1,0:T(8,128)(2,1)} custom-call(s32[1]{0:T(128)} %bitcast.idx_ref, bf16[256,512]{1,0:T(8,128)(2,1)} %copy-done, bf16[512,512]{1,0:T(8,128)(2,1)} %refs_0_.1, bf16[512,512]{1,0:T(8,128)(2,1)} %get-tuple-element.23.refs_1_, bf16[512,512]{1,0:T(8,128)(2,1)} %copy-done.3, bf16[512,512]{1,0:T(8,128)(2,1)} %get-tuple-element.22.refs_3_, ...), custom_call_target="tpu_custom_call" | custom-call | flops 1073741824 | bytes 6291456 | tf_op jit(solution)/shard_map/input_product/pallas_call | solution.py:283
  (90 shorter events, 33.7 us)
Async XLA Ops:
  2.4 16.4 %collective-permute-start = (bf16[528,512]{1,0:T(8,128)(2,1)S(1)}, bf16[528,512]{1,0:T(8,128)(2,1)S(1)}, u32[]{:S(2)}, u32[]{:S(2)}) collective-permute-start(bf16[528,512]{1,0:T(8,128)(2,1)S(1)} %fusion.3.refs_3_.refs_9_), channel_id=1, source_target_pairs={{0,2},{1,3},{2,4},{3,5},{4,6},{5,7},{8,10},{9,11},{10,12},{11,13},... | collective-permute-start | bytes 1622024 | tf_op jit(solution)/shard_map/ppermute | solution.py:222
  7.3 24.0 %collective-permute-start.1 = (bf16[528,512]{1,0:T(8,128)(2,1)S(1)}, bf16[528,512]{1,0:T(8,128)(2,1)S(1)}, u32[]{:S(2)}, u32[]{:S(2)}) collective-permute-start(bf16[528,512]{1,0:T(8,128)(2,1)S(1)} %fusion.3.refs_3_.refs_9_), channel_id=1, source_target_pairs={{0,4},{1,5},{2,6},{3,7},{8,12},{9,13},{10,14},{11,15},{16,20},{17,... | collective-permute-start | bytes 1622024 | tf_op jit(solution)/shard_map/ppermute | solution.py:222
  10.7 20.6 %collective-permute-start.2 = (bf16[528,512]{1,0:T(8,128)(2,1)S(1)}, bf16[528,512]{1,0:T(8,128)(2,1)S(1)}, u32[]{:S(2)}, u32[]{:S(2)}) collective-permute-start(bf16[528,512]{1,0:T(8,128)(2,1)S(1)} %fusion.3.refs_3_.refs_9_), channel_id=1, source_target_pairs={{0,1},{1,0},{2,3},{3,2},{4,5},{5,4},{6,7},{7,6},{8,9},{9,8},{10,11... | collective-permute-start | bytes 1622024 | tf_op jit(solution)/shard_map/ppermute | solution.py:226
  18.8 12.5 %collective-permute-start.3 = (bf16[528,512]{1,0:T(8,128)(2,1)S(1)}, bf16[528,512]{1,0:T(8,128)(2,1)S(1)}, u32[]{:S(2)}, u32[]{:S(2)}) collective-permute-start(bf16[528,512]{1,0:T(8,128)(2,1)S(1)} %collective-permute-done.refs_4_.refs_10_), channel_id=1, source_target_pairs={{0,1},{1,0},{2,3},{3,2},{4,5},{5,4},{6,7},{7,6},{8,9},{9,8},{10,11... | collective-permute-start | bytes 1622024 | tf_op jit(solution)/shard_map/ppermute | solution.py:226
  44.8 8.2 %collective-permute-start.5 = (bf16[3,512,512]{2,1,0:T(8,128)(2,1)}, bf16[3,512,512]{2,1,0:T(8,128)(2,1)S(1)}, u32[]{:S(2)}, u32[]{:S(2)}) collective-permute-start(bf16[3,512,512]{2,1,0:T(8,128)(2,1)} %get-tuple-element.9), channel_id=1, source_target_pairs={{0,1},{1,0},{2,3},{3,2},{4,5},{5,4},{6,7},{7,6},{8,9},{9,8},{10,11... | collective-permute-start | bytes 4718600 | tf_op jit(solution)/shard_map/ppermute | solution.py:226
  54.9 16.1 %collective-permute-start.6 = (bf16[512,512]{1,0:T(8,128)(2,1)S(1)}, bf16[512,512]{1,0:T(8,128)(2,1)S(1)}, u32[]{:S(2)}, u32[]{:S(2)}) collective-permute-start(bf16[512,512]{1,0:T(8,128)(2,1)S(1)} %get-tuple-element.10), channel_id=1, source_target_pairs={{2,0},{3,1},{4,2},{5,3},{6,4},{7,5},{10,8},{11,9},{12,10},{13,11},... | collective-permute-start | bytes 1572872 | tf_op jit(solution)/shard_map/ppermute | solution.py:222
  56.3 21.7 %collective-permute-start.7 = (bf16[512,512]{1,0:T(8,128)(2,1)S(1)}, bf16[512,512]{1,0:T(8,128)(2,1)S(1)}, u32[]{:S(2)}, u32[]{:S(2)}) collective-permute-start(bf16[512,512]{1,0:T(8,128)(2,1)S(1)} %get-tuple-element.11), channel_id=1, source_target_pairs={{4,0},{5,1},{6,2},{7,3},{12,8},{13,9},{14,10},{15,11},{20,16},{21,... | collective-permute-start | bytes 1572872 | tf_op jit(solution)/shard_map/ppermute | solution.py:222
  80.3 18.4 %collective-permute-start.19 = (bf16[256,512]{1,0:T(8,128)(2,1)S(1)}, bf16[256,512]{1,0:T(8,128)(2,1)S(1)}, u32[]{:S(2)}, u32[]{:S(2)}) collective-permute-start(bf16[256,512]{1,0:T(8,128)(2,1)S(1)} %get-tuple-element.31.delta_ref.refs_8_), channel_id=1, source_target_pairs={{0,2},{1,3},{2,0},{3,1},{4,6},{5,7},{6,4},{7,5},{8,10},{9,11},{10,... | collective-permute-start | bytes 786440 | tf_op jit(solution)/shard_map/ppermute | solution.py:226
  91.6 14.8 %collective-permute-start.20 = (bf16[256,512]{1,0:T(8,128)(2,1)S(1)}, bf16[256,512]{1,0:T(8,128)(2,1)S(1)}, u32[]{:S(2)}, u32[]{:S(2)}) collective-permute-start(bf16[256,512]{1,0:T(8,128)(2,1)S(1)} %get-tuple-element.31.delta_ref.refs_8_), channel_id=1, source_target_pairs={{0,4},{1,5},{2,6},{3,7},{4,0},{5,1},{6,2},{7,3},{8,12},{9,13},{10,... | collective-permute-start | bytes 786440 | tf_op jit(solution)/shard_map/ppermute | solution.py:226
  91.6 14.8 %collective-permute-start.21 = (bf16[256,512]{1,0:T(8,128)(2,1)S(1)}, bf16[256,512]{1,0:T(8,128)(2,1)S(1)}, u32[]{:S(2)}, u32[]{:S(2)}) collective-permute-start(bf16[256,512]{1,0:T(8,128)(2,1)S(1)} %get-tuple-element.31.delta_ref.refs_8_), channel_id=1, source_target_pairs={{0,6},{1,7},{2,4},{3,5},{4,2},{5,3},{6,0},{7,1},{8,14},{9,15},{10,... | collective-permute-start | bytes 786440 | tf_op jit(solution)/shard_map/ppermute | solution.py:226
  93.0 22.6 %collective-permute-start.8 = (bf16[512,512]{1,0:T(8,128)(2,1)S(1)}, bf16[512,512]{1,0:T(8,128)(2,1)S(1)}, u32[]{:S(2)}, u32[]{:S(2)}) collective-permute-start(bf16[512,512]{1,0:T(8,128)(2,1)S(1)} %copy-done.2), channel_id=1, source_target_pairs={{0,2},{1,3},{2,0},{3,1},{4,6},{5,7},{6,4},{7,5},{8,10},{9,11},{10,... | collective-permute-start | bytes 1572872 | tf_op jit(solution)/shard_map/ppermute | solution.py:226
  95.1 32.6 %collective-permute-start.9 = (bf16[512,512]{1,0:T(8,128)(2,1)S(1)}, bf16[512,512]{1,0:T(8,128)(2,1)S(1)}, u32[]{:S(2)}, u32[]{:S(2)}) collective-permute-start(bf16[512,512]{1,0:T(8,128)(2,1)S(1)} %copy-done.2), channel_id=1, source_target_pairs={{0,4},{1,5},{2,6},{3,7},{4,0},{5,1},{6,2},{7,3},{8,12},{9,13},{10,... | collective-permute-start | bytes 1572872 | tf_op jit(solution)/shard_map/ppermute | solution.py:226
  98.7 28.9 %collective-permute-start.10 = (bf16[512,512]{1,0:T(8,128)(2,1)S(1)}, bf16[512,512]{1,0:T(8,128)(2,1)S(1)}, u32[]{:S(2)}, u32[]{:S(2)}) collective-permute-start(bf16[512,512]{1,0:T(8,128)(2,1)S(1)} %copy-done.2), channel_id=1, source_target_pairs={{0,6},{1,7},{2,4},{3,5},{4,2},{5,3},{6,0},{7,1},{8,14},{9,15},{10,... | collective-permute-start | bytes 1572872 | tf_op jit(solution)/shard_map/ppermute | solution.py:226
  107.5 38.8 %collective-permute-start.22 = (bf16[4,256,512]{2,1,0:T(8,128)(2,1)}, bf16[4,256,512]{2,1,0:T(8,128)(2,1)}, u32[]{:S(2)}, u32[]{:S(2)}) collective-permute-start(bf16[4,256,512]{2,1,0:T(8,128)(2,1)} %pad_maximum_fusion.1), channel_id=1, source_target_pairs={{0,1},{1,0},{2,3},{3,2},{4,5},{5,4},{6,7},{7,6},{8,9},{9,8},{10,11... | collective-permute-start | bytes 3145736 | tf_op jit(solution)/shard_map/ppermute | solution.py:226
  129.3 70.3 %collective-permute-start.11 = (bf16[4,512,512]{2,1,0:T(8,128)(2,1)}, bf16[4,512,512]{2,1,0:T(8,128)(2,1)}, u32[]{:S(2)}, u32[]{:S(2)}) collective-permute-start(bf16[4,512,512]{2,1,0:T(8,128)(2,1)} %pad_maximum_fusion), channel_id=1, source_target_pairs={{0,1},{1,0},{2,3},{3,2},{4,5},{5,4},{6,7},{7,6},{8,9},{9,8},{10,11... | collective-permute-start | bytes 6291464 | tf_op jit(solution)/shard_map/ppermute | solution.py:226
  131.4 9.2 %collective-permute-start.13 = (bf16[256,512]{1,0:T(8,128)(2,1)S(1)}, bf16[256,512]{1,0:T(8,128)(2,1)S(1)}, u32[]{:S(2)}, u32[]{:S(2)}) collective-permute-start(bf16[256,512]{1,0:T(8,128)(2,1)S(1)} %get-tuple-element.16), channel_id=1, source_target_pairs={{0,2},{1,3},{2,0},{3,1},{4,6},{5,7},{6,4},{7,5},{8,10},{9,11},{10,... | collective-permute-start | bytes 786440 | tf_op jit(solution)/shard_map/ppermute | solution.py:226
  131.7 13.6 %collective-permute-start.14 = (bf16[256,512]{1,0:T(8,128)(2,1)S(1)}, bf16[256,512]{1,0:T(8,128)(2,1)S(1)}, u32[]{:S(2)}, u32[]{:S(2)}) collective-permute-start(bf16[256,512]{1,0:T(8,128)(2,1)S(1)} %get-tuple-element.15), channel_id=1, source_target_pairs={{0,3},{1,2},{2,1},{3,0},{4,7},{5,6},{6,5},{7,4},{8,11},{9,10},{10,... | collective-permute-start | bytes 786440 | tf_op jit(solution)/shard_map/ppermute | solution.py:226
  134.1 16.2 %collective-permute-start.15 = (bf16[256,512]{1,0:T(8,128)(2,1)S(1)}, bf16[256,512]{1,0:T(8,128)(2,1)S(1)}, u32[]{:S(2)}, u32[]{:S(2)}) collective-permute-start(bf16[256,512]{1,0:T(8,128)(2,1)S(1)} %get-tuple-element.14), channel_id=1, source_target_pairs={{0,4},{1,5},{2,6},{3,7},{4,0},{5,1},{6,2},{7,3},{8,12},{9,13},{10,... | collective-permute-start | bytes 786440 | tf_op jit(solution)/shard_map/ppermute | solution.py:226
  140.5 9.8 %collective-permute-start.16 = (bf16[256,512]{1,0:T(8,128)(2,1)S(1)}, bf16[256,512]{1,0:T(8,128)(2,1)S(1)}, u32[]{:S(2)}, u32[]{:S(2)}) collective-permute-start(bf16[256,512]{1,0:T(8,128)(2,1)S(1)} %get-tuple-element.13), channel_id=1, source_target_pairs={{0,5},{1,4},{2,7},{3,6},{4,1},{5,0},{6,3},{7,2},{8,13},{9,12},{10,... | collective-permute-start | bytes 786440 | tf_op jit(solution)/shard_map/ppermute | solution.py:226
  145.2 10.1 %collective-permute-start.17 = (bf16[256,512]{1,0:T(8,128)(2,1)S(1)}, bf16[256,512]{1,0:T(8,128)(2,1)S(1)}, u32[]{:S(2)}, u32[]{:S(2)}) collective-permute-start(bf16[256,512]{1,0:T(8,128)(2,1)S(1)} %get-tuple-element.19), channel_id=1, source_target_pairs={{0,6},{1,7},{2,4},{3,5},{4,2},{5,3},{6,0},{7,1},{8,14},{9,15},{10,... | collective-permute-start | bytes 786440 | tf_op jit(solution)/shard_map/ppermute | solution.py:226
  146.3 13.9 %collective-permute-start.18 = (bf16[256,512]{1,0:T(8,128)(2,1)S(1)}, bf16[256,512]{1,0:T(8,128)(2,1)S(1)}, u32[]{:S(2)}, u32[]{:S(2)}) collective-permute-start(bf16[256,512]{1,0:T(8,128)(2,1)S(1)} %get-tuple-element.12), channel_id=1, source_target_pairs={{0,7},{1,6},{2,5},{3,4},{4,3},{5,2},{6,1},{7,0},{8,15},{9,14},{10,... | collective-permute-start | bytes 786440 | tf_op jit(solution)/shard_map/ppermute | solution.py:226
  166.3 8.5 %collective-permute-start.23 = (bf16[256,512]{1,0:T(8,128)(2,1)S(1)}, bf16[256,512]{1,0:T(8,128)(2,1)S(1)}, u32[]{:S(2)}, u32[]{:S(2)}) collective-permute-start(bf16[256,512]{1,0:T(8,128)(2,1)S(1)} %dynamic-slice_convert_fusion), channel_id=1, source_target_pairs={{0,8},{8,0},{16,24},{24,16},{1,9},{9,1},{17,25},{25,17},{2,10},{10... | collective-permute-start | bytes 786440 | tf_op jit(solution)/shard_map/ppermute | solution.py:226
  175.9 23.6 %collective-permute-start.24 = (bf16[256,512]{1,0:T(8,128)(2,1)S(1)}, bf16[256,512]{1,0:T(8,128)(2,1)S(1)}, u32[]{:S(2)}, u32[]{:S(2)}) collective-permute-start(bf16[256,512]{1,0:T(8,128)(2,1)S(1)} %add_convert_fusion.3), channel_id=1, source_target_pairs={{0,16},{8,24},{16,0},{24,8},{1,17},{9,25},{17,1},{25,9},{2,18},{10... | collective-permute-start | bytes 786440 | tf_op jit(solution)/shard_map/ppermute | solution.py:226
  199.6 8.3 %collective-permute-start.25 = (bf16[256,512]{1,0:T(8,128)(2,1)S(1)}, bf16[256,512]{1,0:T(8,128)(2,1)S(1)}, u32[]{:S(2)}, u32[]{:S(2)}) collective-permute-start(bf16[256,512]{1,0:T(8,128)(2,1)S(1)} %add_convert_fusion.2), channel_id=1, source_target_pairs={{0,8},{8,0},{16,24},{24,16},{1,9},{9,1},{17,25},{25,17},{2,10},{10... | collective-permute-start | bytes 786440 | tf_op jit(solution)/shard_map/ppermute | solution.py:226
  (24 other events, 319.4 us)

commit v2 on v1

--- a/solution.py
+++ b/solution.py
@@ -7,6 +7,7 @@
 from jax.experimental import pallas as pl
 from jax.experimental.pallas import tpu as pltpu
 from jax.sharding import PartitionSpec as P
+
 
 HQ = 16
 KVH = 4
@@ -31,17 +32,17 @@
     return lax.dot_general(a, b, (((0,), (0,)), ((), ())), preferred_element_type=F32)
 
 
-def attend_kernel(chips_back, tok, idx_ref, *refs):
-    blocks = chips_back + 1
-    slots = 2 * blocks
+def attend_kernel(blocks, distances, tok, idx_ref, *refs):
+    chips_back = blocks - 1
+    count = len(distances)
     q_ref, grad_ref, out_ref = refs[:3]
-    same_refs = refs[3 : 3 + blocks]
-    sib_refs = refs[3 + blocks : 3 + 2 * blocks]
-    same_seg = refs[3 + 2 * blocks : 3 + 3 * blocks]
-    sib_seg = refs[3 + 3 * blocks : 3 + 4 * blocks]
-    dq_ref, same_out, sib_out = refs[3 + 4 * blocks : 6 + 4 * blocks]
+    same_refs = refs[3 : 3 + count]
+    sib_refs = refs[3 + count : 3 + 2 * count]
+    same_seg = refs[3 + 2 * count : 3 + 3 * count]
+    sib_seg = refs[3 + 3 * count : 3 + 4 * count]
+    dq_ref, same_out, sib_out = refs[3 + 4 * count : 6 + 4 * count]
     (win, key_t, q4, g4, exp_s, max_s, acc, dq_t, prob_s, ds_s, low_s, lo_s) = refs[
-        6 + 4 * blocks :
+        6 + 4 * count :
     ]
     head = pl.program_id(0)
     here = idx_ref[0]
@@ -60,25 +61,29 @@
     @pl.when(head == 0)
     def _():
         mine = same_seg[0][0:1, 0:tok].astype(F32)
-        count = jnp.zeros((1, tok), F32)
-        for d in range(blocks):
-            for which, seg in ((core, same_seg[d]), (1 - core, sib_seg[d])):
+        total = jnp.zeros((1, tok), F32)
+        for d, serves, *segs in zip(*zip(*distances), same_seg, sib_seg):
+            valid = (serves(chip) & (chip >= d)).astype(F32)
+            for seg in segs:
                 row = seg[0:1, 0:tok].astype(F32)
                 column = jnp.broadcast_to(row, (tok, tok)).T
                 below = jnp.sum(jnp.where(column < mine, 1.0, 0.0), axis=0, keepdims=True)
-                valid = (chip >= d).astype(F32)
-                count = count + below * valid
-        start = count.astype(jnp.int32) + jnp.maximum(base0, 0)
+                total = total + below * valid
+        start = total.astype(jnp.int32) + jnp.maximum(base0, 0)
         query_pos = here * tok + lax.broadcasted_iota(jnp.int32, (1, tok), 1)
         low = jnp.maximum(start, query_pos - (W - 1))
         low_s[...] = jnp.broadcast_to(low, low_s.shape)
         lo_s[0] = lax.div(jnp.min(low.astype(F32)).astype(jnp.int32) - base0, tok)
 
-    for d in range(blocks):
-        for which, ref in ((core, same_refs[d]), (1 - core, sib_refs[d])):
-            slot = slot_of(d, which)
-            win[slot] = ref[...]
-            key_t[slot] = ref[0:tok, :].T
+    for d, serves, same_ref, sib_ref in zip(*zip(*distances), same_refs, sib_refs):
+
+        @pl.when(serves(chip))
+        def _(d=d, same_ref=same_ref, sib_ref=sib_ref):
+            for which, ref in ((core, same_ref), (1 - core, sib_ref)):
+                slot = slot_of(d, which)
+                win[slot] = ref[...]
+                key_t[slot] = ref[0:tok, :].T
+
     acc[...] = jnp.zeros_like(acc)
     dq_t[...] = jnp.zeros_like(dq_t)
     deltas = []
@@ -144,10 +149,11 @@
         sib_out[d] = acc[slot_of(d, 1 - core)].astype(BF16)
 
 
-def attend(index, query, grad, output, same, sibling):
+def attend(index, query, grad, output, distances, same, sibling):
     tok = query.shape[0]
-    blocks = len(same)
+    blocks = 1 + max(d for d, _ in distances)
     slots = 2 * blocks
+    count = len(same) + len(sibling)
     width = KVH * DH
     wide = GROUP * DH
     rows = GROUP * tok
@@ -157,11 +163,11 @@
     part_spec = pl.BlockSpec((blocks, 2 * tok, DH), lambda g, s: (0, 0, g))
     pairs = tok * (blocks * 2 - 1) * tok * HQ
     return pl.pallas_call(
-        functools.partial(attend_kernel, blocks - 1, tok),
+        functools.partial(attend_kernel, blocks, distances, tok),
         grid_spec=pltpu.PrefetchScalarGridSpec(
             num_scalar_prefetch=1,
             grid=(KVH,),
-            in_specs=[head_spec] * 3 + [kv_spec] * slots + [seg_spec] * slots,
+            in_specs=[head_spec] * 3 + [kv_spec] * count + [seg_spec] * count,
             out_specs=[head_spec, part_spec, part_spec],
             scratch_shapes=[
                 pltpu.VMEM((slots, 2 * tok, DH), BF16),
@@ -190,22 +196,24 @@
     )(index, query, grad, output, *same, *sibling, *same, *sibling)
 
 
-def weight_kernel(count, *refs):
-    out_ref = refs[2 * count]
+def weight_kernel(count, idx_ref, rows_ref, *refs):
+    out_ref = refs[count]
     for s in range(count):
-        part = tn_dot(refs[s][...], refs[count + s][...])
+        part = tn_dot(rows_ref[idx_ref[0] ^ s], refs[s][...])
         if s == 0:
             out_ref[...] = part
         else:
             out_ref[...] += part
 
 
-def weight_product(rows, deltas):
-    count = len(rows)
-    tok, depth = rows[0].shape
+def weight_product(index, rows, deltas):
+    count, tok, depth = rows.shape
     width = deltas[0].shape[1]
+    vmem = pl.BlockSpec(memory_space=pltpu.VMEM)
     return pl.pallas_call(
         functools.partial(weight_kernel, count),
+        in_specs=[pl.BlockSpec(memory_space=pltpu.SMEM)] + [vmem] * (1 + count),
+        out_specs=vmem,
         out_shape=jax.ShapeDtypeStruct((depth, width), F32),
         cost_estimate=pl.CostEstimate(
             flops=2 * count * tok * depth * width,
@@ -213,7 +221,29 @@
             transcendentals=0,
         ),
         name="weight_product",
-    )(*rows, *deltas)
+    )(index, rows, *deltas)
+
+
+def split_kernel(in_ref, out_ref):
+    out_ref[0] = in_ref[...]
+
+
+def split_columns(block, count):
+    rows, columns = block.shape
+    depth = columns // count
+    if depth % 128:
+        return block.reshape(rows, count, depth).transpose(1, 0, 2)
+    return pl.pallas_call(
+        split_kernel,
+        grid=(count,),
+        in_specs=[pl.BlockSpec((rows, depth), lambda j: (0, j))],
+        out_specs=pl.BlockSpec((1, rows, depth), lambda j: (j, 0, 0)),
+        out_shape=jax.ShapeDtypeStruct((count, rows, depth), block.dtype),
+        cost_estimate=pl.CostEstimate(
+            flops=0, bytes_accessed=4 * rows * columns, transcendentals=0
+        ),
+        name="split_columns",
+    )(block)
 
 
 def shifted(block, axis, distance):
@@ -222,15 +252,42 @@
     return lax.ppermute(block, axis, route)
 
 
+def behind(own, axis, chips_back):
+    def everyone(chip):
+        return chip >= 0
+
+    size = lax.axis_size(axis)
+    here = lax.axis_index(axis)
+    if size == 8 and chips_back == 2:
+        over_y = lax.ppermute(own, axis, [(i, i + 4) for i in range(4)])
+        over_x = lax.ppermute(own, axis, [(0, 2), (1, 3), (4, 6), (5, 7), (3, 1)])
+        handed = lax.ppermute(jnp.where(here >= 4, over_y, over_x), axis, [(6, 4), (1, 5)])
+        return [own, over_y, over_x, handed], (
+            (0, everyone),
+            (2, everyone),
+            (1, lambda chip: chip != 2),
+            (1, lambda chip: chip == 2),
+        )
+    same, distances = [own], [(0, everyone)]
+    for d in range(1, chips_back + 1):
+        same.append(shifted(own, axis, 2 * d))
+        distances.append((d, everyone))
+    return same, tuple(distances)
+
+
 def swapped(block, axis, mask):
     return lax.ppermute(block, axis, [(i, i ^ mask) for i in range(lax.axis_size(axis))])
 
 
 def gathered(block, axis):
     size = lax.axis_size(axis)
-    even = [block if m == 0 else swapped(block, axis, m) for m in range(0, size, 2)]
-    odd = swapped(jnp.stack(even), axis, 1)
-    return [(even[m // 2] if m % 2 == 0 else odd[m // 2]) for m in range(size)]
+    even = [block]
+    for m in range(2, size, 2):
+        even.append(swapped(block, axis, m))
+    blocks = []
+    for block in even:
+        blocks += [block, swapped(block, axis, 1)]
+    return blocks
 
 
 def summed(part, axis):
@@ -249,7 +306,8 @@
         part = keep + swapped(send.astype(BF16), axis, mask).astype(F32)
     if masks:
         low = part.astype(BF16)
-        part = low.astype(F32) + swapped(low, axis, masks[-1]).astype(F32)
+        other = swapped(low, axis, masks[-1])
+        part = low.astype(F32) + other.astype(F32)
     for mask in reversed(masks[:-1]):
         low = part.astype(BF16)
         other = swapped(low, axis, mask)
@@ -307,22 +365,19 @@
     size = lax.axis_size("ctx")
     here = lax.axis_index("ctx")
     tok = query_states.shape[1]
-    depth = value_weight.shape[0]
     width = KVH * DH
     index = here.astype(jnp.int32).reshape(1)
     reach = min(W, size * tok // 2)
     chips_back = -(-(-(-(reach - 1) // tok)) // 2)
     seg = jnp.pad(segment_ids.astype(BF16), ((0, SEG_ROWS - 1), (0, width - tok)))
     own = jnp.concatenate([key_states[0], value_states[0], seg], axis=0)
-    same = [own] + [shifted(own, "ctx", 2 * d) for d in range(1, chips_back + 1)]
+    same, distances = behind(own, "ctx", chips_back)
     sibling = [swapped(block, "ctx", 1) for block in same]
     query_grad, same_part, sib_part = attend(
-        index, query_states[0], out_grad[0], attention_out[0], same, sibling
+        index, query_states[0], out_grad[0], attention_out[0], distances, same, sibling
     )
-    rows = [
-        lax.dynamic_slice_in_dim(inputs[0], (here ^ m) * depth, depth, 1) for m in range(size)
-    ]
-    rows = [rows[0]] + [swapped(rows[m], "ctx", m) for m in range(1, size)]
+    rows = split_columns(inputs[0], size)
+    rows = lax.all_to_all(rows, "ctx", 0, 0, tiled=True)
     weights = gathered(value_weight, "ctx")
 
     part = swapped(sib_part, "ctx", 1)
@@ -334,7 +389,8 @@
     key_grad = low[:tok]
     value_delta = low[tok:]
     deltas = gathered(value_delta, "ctx")
-    weight_grad = summed(weight_product(rows, deltas), "dp")
+    weight_part = weight_product(index, rows, deltas)
+    weight_grad = summed(weight_part, "dp")
     input_grad = input_product(index, value_delta, weights)
     return (query_grad[None], key_grad[None], input_grad[None], weight_grad)
 

time: 210 us -> 184 us (0.88)
  waiting for transfers between devices: 118 us -> 79.1 us
  starting transfers between devices: 49.2 us -> 65.4 us
  local copies, waits for them, and re-layouts: 10.5 us -> 2.72 us
  Pallas kernels: 20 us -> 26.3 us
    ppermute x22, waiting for transfers between devices: 77.4 us -> 35.2 us  [swapped(): lax.ppermute(block, axis, [(i, i ^ mask) for i in range(lax.axis_size(axi...]
    all_to_all x0 -> x1, starting transfers between devices: none -> 20 us  [on_device(): rows = lax.all_to_all(rows, 'ctx', 0, 0, tiled=True)]
    ppermute x0 -> x3, waiting for transfers between devices: none -> 11.2 us  [the longest x1 8.04 us: behind(): over_y = lax.ppermute(own, axis, [(i, i + 4) for i in range(4)])]
    ppermute x0 -> x3, starting transfers between devices: none -> 9.06 us  [the longest x1 4.93 us: behind(): over_y = lax.ppermute(own, axis, [(i, i + 4) for i in range(4)])]
    ppermute x4 -> x2, starting transfers between devices: 11 us -> 2.58 us  [shifted(): return lax.ppermute(block, axis, route)]
    ppermute x4 -> x2, waiting for transfers between devices: 40.8 us -> 32.6 us  [shifted(): return lax.ppermute(block, axis, route)]
    pallas_call x2 -> x3, Pallas kernels: 15.1 us -> 21.4 us  [the longest x1 11.4 us: attend(): pl.pallas_call(functools.partial(attend_kernel, blocks, distances, tok),...]
    squeeze x2 -> x0, local copies, waits for them, and re-layouts: 5.14 us -> none  [gathered(): return [even[m // 2] if m % 2 == 0 else odd[m // 2] for m in range(size)]]
  transfers between devices with their start and end apart: 26 -> 28, of which waited for: 18 -> 15; matrix products, arithmetic and copies ran while one was open for 5% -> 3% of each run, Pallas kernels for 4% -> 6%
where the time goes in v2:
time: 184 us; the launch traced here: 183 us
  waiting for transfers between devices  79.1 us (43%)
  starting transfers between devices  65.4 us (36%)
  Pallas kernels  26.3 us (14%)
  other arithmetic  8.94 us (5%)
  local copies, waits for them, and re-layouts  2.72 us (1%)
    ppermute x22, waiting for transfers between devices, swapped(): lax.ppermute(block, axis, [(i, i ^ mask) for i in range(lax.axis_size(axi...  35.2 us
    ppermute x22, starting transfers between devices, swapped(): lax.ppermute(block, axis, [(i, i ^ mask) for i in range(lax.axis_size(axi...  33.8 us
    ppermute x2, waiting for transfers between devices, shifted(): return lax.ppermute(block, axis, route)  32.6 us
    all_to_all x1, starting transfers between devices, on_device(): rows = lax.all_to_all(rows, 'ctx', 0, 0, tiled=True)  20 us
    pallas_call x1, Pallas kernels, attend(): pl.pallas_call(functools.partial(attend_kernel, blocks, distances, tok),...  11.4 us
    ppermute x1, waiting for transfers between devices, behind(): over_y = lax.ppermute(own, axis, [(i, i + 4) for i in range(4)])  8.04 us
    pallas_call x1, Pallas kernels, split_columns(): pl.pallas_call(split_kernel, grid=(count,), in_specs=[pl.BlockSpec((rows,...  5.63 us
    ppermute x1, starting transfers between devices, behind(): over_y = lax.ppermute(own, axis, [(i, i + 4) for i in range(4)])  4.93 us
  transfers between devices with their start and end apart: 28, of which 15 were waited for; matrix products, arithmetic and copies ran while one was open for 3% of the time, Pallas kernels for 6%

profile of v2, /device:TPU:0, one launch (start us, length us, event | category | flops | bytes accessed | tf_op | source)
XLA Modules:
  0.0 183.3 jit_solution(5120346344918342925)
XLA Ops:
  2.4 4.9 %collective-permute-start = (bf16[528,512]{1,0:T(8,128)(2,1)S(1)}, bf16[528,512]{1,0:T(8,128)(2,1)S(1)}, u32[]{:S(2)}, u32[]{:S(2)}) collective-permute-start(bf16[528,512]{1,0:T(8,128)(2,1)S(1)} %fusion.3.refs_3_.refs_11_), channel_id=1, source_target_pairs={{0,4},{1,5},{2,6},{3,7},{8,12},{9,13},{10,14},{11,15},{16,20},{17,... | collective-permute-start | bytes 1622024 | tf_op jit(solution)/shard_map/ppermute | solution.py:262
  7.3 3.4 %collective-permute-start.1 = (bf16[528,512]{1,0:T(8,128)(2,1)S(1)}, bf16[528,512]{1,0:T(8,128)(2,1)S(1)}, u32[]{:S(2)}, u32[]{:S(2)}) collective-permute-start(bf16[528,512]{1,0:T(8,128)(2,1)S(1)} %fusion.3.refs_3_.refs_11_), channel_id=1, source_target_pairs={{0,2},{1,3},{4,6},{5,7},{3,1},{8,10},{9,11},{12,14},{13,15},{11,9}... | collective-permute-start | bytes 1622024 | tf_op jit(solution)/shard_map/ppermute | solution.py:263
  10.8 8.0 %collective-permute-done.refs_4_.refs_12_ = bf16[528,512]{1,0:T(8,128)(2,1)S(1)} collective-permute-done((bf16[528,512]{1,0:T(8,128)(2,1)S(1)}, bf16[528,512]{1,0:T(8,128)(2,1)S(1)}, u32[]{:S(2)}, u32[]{:S(2)}) %collective-permute-start) | collective-permute-done | bytes 540704 | tf_op jit(solution)/shard_map/ppermute | solution.py:262
  18.8 3.2 %collective-permute-done.1.refs_5_.refs_13_ = bf16[528,512]{1,0:T(8,128)(2,1)S(1)} collective-permute-done((bf16[528,512]{1,0:T(8,128)(2,1)S(1)}, bf16[528,512]{1,0:T(8,128)(2,1)S(1)}, u32[]{:S(2)}, u32[]{:S(2)}) %collective-permute-start.1) | collective-permute-done | bytes 540704 | tf_op jit(solution)/shard_map/ppermute | solution.py:263
  23.4 5.2 %collective-permute-start.6 = (bf16[528,512]{1,0:T(8,128)(2,1)S(1)}, bf16[528,512]{1,0:T(8,128)(2,1)S(1)}, u32[]{:S(2)}, u32[]{:S(2)}) collective-permute-start(bf16[528,512]{1,0:T(8,128)(2,1)S(1)} %collective-permute-done.2.refs_6_.refs_14_), channel_id=1, source_target_pairs={{0,1},{1,0},{2,3},{3,2},{4,5},{5,4},{6,7},{7,6},{8,9},{9,8},{10,11... | collective-permute-start | bytes 1622024 | tf_op jit(solution)/shard_map/ppermute | solution.py:279
  28.6 1.5 collective-permute-done.6.refs_10_.refs_18_
  31.0 11.4 %attend.1 = (bf16[256,2048]{1,0:T(8,128)(2,1)}, f32[3,512,512]{2,1,0:T(8,128)}, bf16[3,512,512]{2,1,0:T(8,128)(2,1)}) custom-call(s32[1]{0:T(128)} %bitcast.idx_ref, bf16[256,2048]{1,0:T(8,128)(2,1)} %bitcast.25, bf16[256,2048]{1,0:T(8,128)(2,1)} %bitcast.26, bf16[256,2048]{1,0:T(8,128)(2,1)} %bitcast.27, bf16[528,512]{1,0:T(8,128)(2,1)} %copy-done.2, ...), custom_call_target="tpu_custom_call" | custom-call | flops 13421772800 | bytes 12582912 | tf_op jit(solution)/shard_map/attend/pallas_call | solution.py:165
  42.4 5.2 %collective-permute-start.7 = (bf16[3,512,512]{2,1,0:T(8,128)(2,1)}, bf16[3,512,512]{2,1,0:T(8,128)(2,1)}, u32[]{:S(2)}, u32[]{:S(2)}) collective-permute-start(bf16[3,512,512]{2,1,0:T(8,128)(2,1)} %get-tuple-element.9), channel_id=1, source_target_pairs={{0,1},{1,0},{2,3},{3,2},{4,5},{5,4},{6,7},{7,6},{8,9},{9,8},{10,11... | collective-permute-start | bytes 4718600 | tf_op jit(solution)/shard_map/ppermute | solution.py:279
  47.6 5.6 %split_columns.1 = bf16[8,256,512]{2,1,0:T(8,128)(2,1)} custom-call(bf16[256,4096]{1,0:T(8,128)(2,1)} %bitcast.21), custom_call_target="tpu_custom_call" | custom-call | bytes 4194304 | tf_op jit(solution)/shard_map/split_columns/pallas_call | solution.py:236
  53.2 20.0 %all-to-all-start = ((bf16[8,256,512]{2,1,0:T(8,128)(2,1)}), bf16[8,256,512]{2,1,0:T(8,128)(2,1)S(1)}, u32[]{:S(2)}, u32[]{:S(2)}) async-start(bf16[8,256,512]{2,1,0:T(8,128)(2,1)} %split_columns.1), calls=%async_computation | async-start | bytes 4194304 | tf_op jit(solution)/shard_map/all_to_all | solution.py:380
  73.2 2.2 %fusion.4 = (bf16[512,512]{1,0:T(8,128)(2,1)S(1)}, bf16[512,512]{1,0:T(8,128)(2,1)S(1)}) fusion(f32[3,512,512]{2,1,0:T(8,128)} %get-tuple-element.8, bf16[3,512,512]{2,1,0:T(8,128)(2,1)} %collective-permute-done.7), kind=kLoop, calls=%fused_computation.9 | loop fusion | flops 1572864 | bytes 4194304 | tf_op jit(solution)/shard_map/convert_element_type | solution.py:386
  78.0 32.2 %collective-permute-done.8 = bf16[512,512]{1,0:T(8,128)(2,1)S(1)} collective-permute-done((bf16[512,512]{1,0:T(8,128)(2,1)S(1)}, bf16[512,512]{1,0:T(8,128)(2,1)S(1)}, u32[]{:S(2)}, u32[]{:S(2)}) %collective-permute-start.8) | collective-permute-done | bytes 524320 | tf_op jit(solution)/shard_map/ppermute | solution.py:252
  110.6 1.7 fusion.2
  113.0 12.2 %collective-permute-start.18 = (bf16[256,512]{1,0:T(8,128)(2,1)S(1)}, bf16[256,512]{1,0:T(8,128)(2,1)S(1)}, u32[]{:S(2)}, u32[]{:S(2)}) collective-permute-start(bf16[256,512]{1,0:T(8,128)(2,1)S(1)} %get-tuple-element.14.delta_ref.refs_0_), channel_id=1, source_target_pairs={{0,2},{1,3},{2,0},{3,1},{4,6},{5,7},{6,4},{7,5},{8,10},{9,11},{10,... | collective-permute-start | bytes 786440 | tf_op jit(solution)/shard_map/ppermute | solution.py:279
  125.2 1.5 collective-permute-start.22
  126.7 5.7 %collective-permute-done.18.refs_2_ = bf16[256,512]{1,0:T(8,128)(2,1)S(1)} collective-permute-done((bf16[256,512]{1,0:T(8,128)(2,1)S(1)}, bf16[256,512]{1,0:T(8,128)(2,1)S(1)}, u32[]{:S(2)}, u32[]{:S(2)}) %collective-permute-start.18) | collective-permute-done | bytes 262176 | tf_op jit(solution)/shard_map/ppermute | solution.py:279
  132.4 5.9 %collective-permute-done.20.refs_4_ = bf16[256,512]{1,0:T(8,128)(2,1)S(1)} collective-permute-done((bf16[256,512]{1,0:T(8,128)(2,1)S(1)}, bf16[256,512]{1,0:T(8,128)(2,1)S(1)}, u32[]{:S(2)}, u32[]{:S(2)}) %collective-permute-start.20) | collective-permute-done | bytes 262176 | tf_op jit(solution)/shard_map/ppermute | solution.py:279
  140.4 4.4 %weight_product.1 = f32[512,512]{1,0:T(8,128)} custom-call(s32[1]{0:T(128)} %bitcast.idx_ref, bf16[8,256,512]{2,1,0:T(8,128)(2,1)} %copy-done, bf16[256,512]{1,0:T(8,128)(2,1)} %copy-done.1, bf16[256,512]{1,0:T(8,128)(2,1)} %collective-permute-done.17.refs_1_, bf16[256,512]{1,0:T(8,128)(2,1)} %copy-done.11, ...), custom_call_target="tpu_custom_call" | custom-call | flops 1073741824 | bytes 5242880 | tf_op jit(solution)/shard_map/weight_product/pallas_call | solution.py:213
  148.7 1.8 collective-permute-start.15
  150.5 4.0 %collective-permute-done.24 = bf16[256,512]{1,0:T(8,128)(2,1)S(1)} collective-permute-done((bf16[256,512]{1,0:T(8,128)(2,1)S(1)}, bf16[256,512]{1,0:T(8,128)(2,1)S(1)}, u32[]{:S(2)}, u32[]{:S(2)}) %collective-permute-start.24) | collective-permute-done | bytes 262176 | tf_op jit(solution)/shard_map/ppermute | solution.py:279
  155.6 2.5 %collective-permute-start.25 = (bf16[256,512]{1,0:T(8,128)(2,1)S(1)}, bf16[256,512]{1,0:T(8,128)(2,1)S(1)}, u32[]{:S(2)}, u32[]{:S(2)}) collective-permute-start(bf16[256,512]{1,0:T(8,128)(2,1)S(1)} %add_convert_fusion.3), channel_id=1, source_target_pairs={{0,16},{8,24},{16,0},{24,8},{1,17},{9,25},{17,1},{25,9},{2,18},{10... | collective-permute-start | bytes 786440 | tf_op jit(solution)/shard_map/ppermute | solution.py:279
  158.1 3.7 %collective-permute-done.11.refs_2_ = bf16[512,512]{1,0:T(8,128)(2,1)S(1)} collective-permute-done((bf16[512,512]{1,0:T(8,128)(2,1)S(1)}, bf16[512,512]{1,0:T(8,128)(2,1)S(1)}, u32[]{:S(2)}, u32[]{:S(2)}) %collective-permute-start.11) | collective-permute-done | bytes 524320 | tf_op jit(solution)/shard_map/ppermute | solution.py:279
  161.8 10.3 %collective-permute-done.13.refs_4_ = bf16[512,512]{1,0:T(8,128)(2,1)S(1)} collective-permute-done((bf16[512,512]{1,0:T(8,128)(2,1)S(1)}, bf16[512,512]{1,0:T(8,128)(2,1)S(1)}, u32[]{:S(2)}, u32[]{:S(2)}) %collective-permute-start.13) | collective-permute-done | bytes 524320 | tf_op jit(solution)/shard_map/ppermute | solution.py:279
  174.9 4.8 %input_product.1 = bf16[256,4096]{1,0:T(8,128)(2,1)} custom-call(s32[1]{0:T(128)} %bitcast.idx_ref, bf16[256,512]{1,0:T(8,128)(2,1)} %copy-done.1, bf16[512,512]{1,0:T(8,128)(2,1)} %refs_0_.1, bf16[512,512]{1,0:T(8,128)(2,1)} %copy-done.9, bf16[512,512]{1,0:T(8,128)(2,1)} %copy-done.6, bf16[512,512]{1,0:T(8,128)(2,1)} %copy-done.10, ...), custom_call_target="tpu_custom_call" | custom-call | flops 1073741824 | bytes 6291456 | tf_op jit(solution)/shard_map/input_product/pallas_call | solution.py:341
  (83 shorter events, 21.1 us)
Async XLA Ops:
  2.4 16.4 %collective-permute-start = (bf16[528,512]{1,0:T(8,128)(2,1)S(1)}, bf16[528,512]{1,0:T(8,128)(2,1)S(1)}, u32[]{:S(2)}, u32[]{:S(2)}) collective-permute-start(bf16[528,512]{1,0:T(8,128)(2,1)S(1)} %fusion.3.refs_3_.refs_11_), channel_id=1, source_target_pairs={{0,4},{1,5},{2,6},{3,7},{8,12},{9,13},{10,14},{11,15},{16,20},{17,... | collective-permute-start | bytes 1622024 | tf_op jit(solution)/shard_map/ppermute | solution.py:262
  7.3 14.6 %collective-permute-start.1 = (bf16[528,512]{1,0:T(8,128)(2,1)S(1)}, bf16[528,512]{1,0:T(8,128)(2,1)S(1)}, u32[]{:S(2)}, u32[]{:S(2)}) collective-permute-start(bf16[528,512]{1,0:T(8,128)(2,1)S(1)} %fusion.3.refs_3_.refs_11_), channel_id=1, source_target_pairs={{0,2},{1,3},{4,6},{5,7},{3,1},{8,10},{9,11},{12,14},{13,15},{11,9}... | collective-permute-start | bytes 1622024 | tf_op jit(solution)/shard_map/ppermute | solution.py:263
  22.7 5.8 %collective-permute-start.3 = (bf16[528,512]{1,0:T(8,128)(2,1)S(1)}, bf16[528,512]{1,0:T(8,128)(2,1)S(1)}, u32[]{:S(2)}, u32[]{:S(2)}) collective-permute-start(bf16[528,512]{1,0:T(8,128)(2,1)S(1)} %fusion.3.refs_3_.refs_11_), channel_id=1, source_target_pairs={{0,1},{1,0},{2,3},{3,2},{4,5},{5,4},{6,7},{7,6},{8,9},{9,8},{10,11... | collective-permute-start | bytes 1622024 | tf_op jit(solution)/shard_map/ppermute | solution.py:279
  22.8 5.8 %collective-permute-start.4 = (bf16[528,512]{1,0:T(8,128)(2,1)S(1)}, bf16[528,512]{1,0:T(8,128)(2,1)S(1)}, u32[]{:S(2)}, u32[]{:S(2)}) collective-permute-start(bf16[528,512]{1,0:T(8,128)(2,1)S(1)} %collective-permute-done.refs_4_.refs_12_), channel_id=1, source_target_pairs={{0,1},{1,0},{2,3},{3,2},{4,5},{5,4},{6,7},{7,6},{8,9},{9,8},{10,11... | collective-permute-start | bytes 1622024 | tf_op jit(solution)/shard_map/ppermute | solution.py:279
  23.3 5.3 %collective-permute-start.5 = (bf16[528,512]{1,0:T(8,128)(2,1)S(1)}, bf16[528,512]{1,0:T(8,128)(2,1)S(1)}, u32[]{:S(2)}, u32[]{:S(2)}) collective-permute-start(bf16[528,512]{1,0:T(8,128)(2,1)S(1)} %collective-permute-done.1.refs_5_.refs_13_), channel_id=1, source_target_pairs={{0,1},{1,0},{2,3},{3,2},{4,5},{5,4},{6,7},{7,6},{8,9},{9,8},{10,11... | collective-permute-start | bytes 1622024 | tf_op jit(solution)/shard_map/ppermute | solution.py:279
  23.4 6.7 %collective-permute-start.6 = (bf16[528,512]{1,0:T(8,128)(2,1)S(1)}, bf16[528,512]{1,0:T(8,128)(2,1)S(1)}, u32[]{:S(2)}, u32[]{:S(2)}) collective-permute-start(bf16[528,512]{1,0:T(8,128)(2,1)S(1)} %collective-permute-done.2.refs_6_.refs_14_), channel_id=1, source_target_pairs={{0,1},{1,0},{2,3},{3,2},{4,5},{5,4},{6,7},{7,6},{8,9},{9,8},{10,11... | collective-permute-start | bytes 1622024 | tf_op jit(solution)/shard_map/ppermute | solution.py:279
  42.4 30.8 %collective-permute-start.7 = (bf16[3,512,512]{2,1,0:T(8,128)(2,1)}, bf16[3,512,512]{2,1,0:T(8,128)(2,1)}, u32[]{:S(2)}, u32[]{:S(2)}) collective-permute-start(bf16[3,512,512]{2,1,0:T(8,128)(2,1)} %get-tuple-element.9), channel_id=1, source_target_pairs={{0,1},{1,0},{2,3},{3,2},{4,5},{5,4},{6,7},{7,6},{8,9},{9,8},{10,11... | collective-permute-start | bytes 4718600 | tf_op jit(solution)/shard_map/ppermute | solution.py:279
  53.2 85.6 %all-to-all-start = ((bf16[8,256,512]{2,1,0:T(8,128)(2,1)}), bf16[8,256,512]{2,1,0:T(8,128)(2,1)S(1)}, u32[]{:S(2)}, u32[]{:S(2)}) async-start(bf16[8,256,512]{2,1,0:T(8,128)(2,1)} %split_columns.1), calls=%async_computation | async-start | bytes 4194304 | tf_op jit(solution)/shard_map/all_to_all | solution.py:380
  75.4 34.8 %collective-permute-start.8 = (bf16[512,512]{1,0:T(8,128)(2,1)S(1)}, bf16[512,512]{1,0:T(8,128)(2,1)S(1)}, u32[]{:S(2)}, u32[]{:S(2)}) collective-permute-start(bf16[512,512]{1,0:T(8,128)(2,1)S(1)} %get-tuple-element.10), channel_id=1, source_target_pairs={{2,0},{3,1},{4,2},{5,3},{6,4},{7,5},{10,8},{11,9},{12,10},{13,11},... | collective-permute-start | bytes 1572872 | tf_op jit(solution)/shard_map/ppermute | solution.py:252
  76.7 33.9 %collective-permute-start.9 = (bf16[512,512]{1,0:T(8,128)(2,1)S(1)}, bf16[512,512]{1,0:T(8,128)(2,1)S(1)}, u32[]{:S(2)}, u32[]{:S(2)}) collective-permute-start(bf16[512,512]{1,0:T(8,128)(2,1)S(1)} %get-tuple-element.11), channel_id=1, source_target_pairs={{4,0},{5,1},{6,2},{7,3},{12,8},{13,9},{14,10},{15,11},{20,16},{21,... | collective-permute-start | bytes 1572872 | tf_op jit(solution)/shard_map/ppermute | solution.py:252
  113.0 19.4 %collective-permute-start.18 = (bf16[256,512]{1,0:T(8,128)(2,1)S(1)}, bf16[256,512]{1,0:T(8,128)(2,1)S(1)}, u32[]{:S(2)}, u32[]{:S(2)}) collective-permute-start(bf16[256,512]{1,0:T(8,128)(2,1)S(1)} %get-tuple-element.14.delta_ref.refs_0_), channel_id=1, source_target_pairs={{0,2},{1,3},{2,0},{3,1},{4,6},{5,7},{6,4},{7,5},{8,10},{9,11},{10,... | collective-permute-start | bytes 786440 | tf_op jit(solution)/shard_map/ppermute | solution.py:279
  125.2 13.1 %collective-permute-start.20 = (bf16[256,512]{1,0:T(8,128)(2,1)S(1)}, bf16[256,512]{1,0:T(8,128)(2,1)S(1)}, u32[]{:S(2)}, u32[]{:S(2)}) collective-permute-start(bf16[256,512]{1,0:T(8,128)(2,1)S(1)} %get-tuple-element.14.delta_ref.refs_0_), channel_id=1, source_target_pairs={{0,4},{1,5},{2,6},{3,7},{4,0},{5,1},{6,2},{7,3},{8,12},{9,13},{10,... | collective-permute-start | bytes 786440 | tf_op jit(solution)/shard_map/ppermute | solution.py:279
  125.2 13.1 %collective-permute-start.22 = (bf16[256,512]{1,0:T(8,128)(2,1)S(1)}, bf16[256,512]{1,0:T(8,128)(2,1)}, u32[]{:S(2)}, u32[]{:S(2)}) collective-permute-start(bf16[256,512]{1,0:T(8,128)(2,1)S(1)} %get-tuple-element.14.delta_ref.refs_0_), channel_id=1, source_target_pairs={{0,6},{1,7},{2,4},{3,5},{4,2},{5,3},{6,0},{7,1},{8,14},{9,15},{10,... | collective-permute-start | bytes 786440 | tf_op jit(solution)/shard_map/ppermute | solution.py:279
  126.7 12.2 %collective-permute-start.17 = (bf16[256,512]{1,0:T(8,128)(2,1)S(1)}, bf16[256,512]{1,0:T(8,128)(2,1)}, u32[]{:S(2)}, u32[]{:S(2)}) collective-permute-start(bf16[256,512]{1,0:T(8,128)(2,1)S(1)} %get-tuple-element.14.delta_ref.refs_0_), channel_id=1, source_target_pairs={{0,1},{1,0},{2,3},{3,2},{4,5},{5,4},{6,7},{7,6},{8,9},{9,8},{10,11... | collective-permute-start | bytes 786440 | tf_op jit(solution)/shard_map/ppermute | solution.py:279
  132.4 6.5 %collective-permute-start.19 = (bf16[256,512]{1,0:T(8,128)(2,1)S(1)}, bf16[256,512]{1,0:T(8,128)(2,1)}, u32[]{:S(2)}, u32[]{:S(2)}) collective-permute-start(bf16[256,512]{1,0:T(8,128)(2,1)S(1)} %collective-permute-done.18.refs_2_), channel_id=1, source_target_pairs={{0,1},{1,0},{2,3},{3,2},{4,5},{5,4},{6,7},{7,6},{8,9},{9,8},{10,11... | collective-permute-start | bytes 786440 | tf_op jit(solution)/shard_map/ppermute | solution.py:279
  145.8 8.6 %collective-permute-start.24 = (bf16[256,512]{1,0:T(8,128)(2,1)S(1)}, bf16[256,512]{1,0:T(8,128)(2,1)S(1)}, u32[]{:S(2)}, u32[]{:S(2)}) collective-permute-start(bf16[256,512]{1,0:T(8,128)(2,1)S(1)} %dynamic-slice_convert_fusion), channel_id=1, source_target_pairs={{0,8},{8,0},{16,24},{24,16},{1,9},{9,1},{17,25},{25,17},{2,10},{10... | collective-permute-start | bytes 786440 | tf_op jit(solution)/shard_map/ppermute | solution.py:279
  147.0 14.8 %collective-permute-start.11 = (bf16[512,512]{1,0:T(8,128)(2,1)S(1)}, bf16[512,512]{1,0:T(8,128)(2,1)S(1)}, u32[]{:S(2)}, u32[]{:S(2)}) collective-permute-start(bf16[512,512]{1,0:T(8,128)(2,1)S(1)} %copy-done.5), channel_id=1, source_target_pairs={{0,2},{1,3},{2,0},{3,1},{4,6},{5,7},{6,4},{7,5},{8,10},{9,11},{10,... | collective-permute-start | bytes 1572872 | tf_op jit(solution)/shard_map/ppermute | solution.py:279
  147.3 24.9 %collective-permute-start.13 = (bf16[512,512]{1,0:T(8,128)(2,1)S(1)}, bf16[512,512]{1,0:T(8,128)(2,1)S(1)}, u32[]{:S(2)}, u32[]{:S(2)}) collective-permute-start(bf16[512,512]{1,0:T(8,128)(2,1)S(1)} %copy-done.5), channel_id=1, source_target_pairs={{0,4},{1,5},{2,6},{3,7},{4,0},{5,1},{6,2},{7,3},{8,12},{9,13},{10,... | collective-permute-start | bytes 1572872 | tf_op jit(solution)/shard_map/ppermute | solution.py:279
  148.7 23.5 %collective-permute-start.15 = (bf16[512,512]{1,0:T(8,128)(2,1)S(1)}, bf16[512,512]{1,0:T(8,128)(2,1)S(1)}, u32[]{:S(2)}, u32[]{:S(2)}) collective-permute-start(bf16[512,512]{1,0:T(8,128)(2,1)S(1)} %copy-done.5), channel_id=1, source_target_pairs={{0,6},{1,7},{2,4},{3,5},{4,2},{5,3},{6,0},{7,1},{8,14},{9,15},{10,... | collective-permute-start | bytes 1572872 | tf_op jit(solution)/shard_map/ppermute | solution.py:279
  155.6 17.1 %collective-permute-start.25 = (bf16[256,512]{1,0:T(8,128)(2,1)S(1)}, bf16[256,512]{1,0:T(8,128)(2,1)S(1)}, u32[]{:S(2)}, u32[]{:S(2)}) collective-permute-start(bf16[256,512]{1,0:T(8,128)(2,1)S(1)} %add_convert_fusion.3), channel_id=1, source_target_pairs={{0,16},{8,24},{16,0},{24,8},{1,17},{9,25},{17,1},{25,9},{2,18},{10... | collective-permute-start | bytes 786440 | tf_op jit(solution)/shard_map/ppermute | solution.py:279
  158.1 15.7 %collective-permute-start.10 = (bf16[512,512]{1,0:T(8,128)(2,1)S(1)}, bf16[512,512]{1,0:T(8,128)(2,1)S(1)}, u32[]{:S(2)}, u32[]{:S(2)}) collective-permute-start(bf16[512,512]{1,0:T(8,128)(2,1)S(1)} %copy-done.5), channel_id=1, source_target_pairs={{0,1},{1,0},{2,3},{3,2},{4,5},{5,4},{6,7},{7,6},{8,9},{9,8},{10,11... | collective-permute-start | bytes 1572872 | tf_op jit(solution)/shard_map/ppermute | solution.py:279
  161.8 12.0 %collective-permute-start.12 = (bf16[512,512]{1,0:T(8,128)(2,1)S(1)}, bf16[512,512]{1,0:T(8,128)(2,1)S(1)}, u32[]{:S(2)}, u32[]{:S(2)}) collective-permute-start(bf16[512,512]{1,0:T(8,128)(2,1)S(1)} %collective-permute-done.11.refs_2_), channel_id=1, source_target_pairs={{0,1},{1,0},{2,3},{3,2},{4,5},{5,4},{6,7},{7,6},{8,9},{9,8},{10,11... | collective-permute-start | bytes 1572872 | tf_op jit(solution)/shard_map/ppermute | solution.py:279
  172.1 2.8 %collective-permute-start.16 = (bf16[512,512]{1,0:T(8,128)(2,1)S(1)}, bf16[512,512]{1,0:T(8,128)(2,1)}, u32[]{:S(2)}, u32[]{:S(2)}) collective-permute-start(bf16[512,512]{1,0:T(8,128)(2,1)S(1)} %collective-permute-done.15.refs_6_), channel_id=1, source_target_pairs={{0,1},{1,0},{2,3},{3,2},{4,5},{5,4},{6,7},{7,6},{8,9},{9,8},{10,11... | collective-permute-start | bytes 1572872 | tf_op jit(solution)/shard_map/ppermute | solution.py:279
  172.7 8.5 %collective-permute-start.26 = (bf16[256,512]{1,0:T(8,128)(2,1)S(1)}, bf16[256,512]{1,0:T(8,128)(2,1)}, u32[]{:S(2)}, u32[]{:S(2)}) collective-permute-start(bf16[256,512]{1,0:T(8,128)(2,1)S(1)} %add_convert_fusion.2), channel_id=1, source_target_pairs={{0,8},{8,0},{16,24},{24,16},{1,9},{9,1},{17,25},{25,17},{2,10},{10... | collective-permute-start | bytes 786440 | tf_op jit(solution)/shard_map/ppermute | solution.py:279
  (22 other events, 139.8 us)
